TPU v7x, 256 devices: a whole 4x4x8 slice. The times are simulated.
256 devices in a mesh: wide: 64 (over z, y, core), lev: 4 (over x).
Axes of the slice: x: 4, y: 4, z: 8, core: 2. Of those that a mesh axis runs over, the one named last changes fastest.
Arguments:
- spec_in: bfloat16 [320, 2, 4, 641], P('wide', None, 'lev'), may hold values from -0.0068359375 to 0.0068359375
- legendre: bfloat16 [320, 641, 1280], P('wide'), may hold values from -4 to 4
- wind: bfloat16 [1280, 4, 2560], P(('wide', 'lev')), may hold values from -6 to 6
- lat_weight: float32 [1280], replicated, may hold values from 1 to 4
- wave_order: int32 [640], replicated, may hold values from 0 to 639, as said below
- lat_order: int32 [1280], replicated, may hold values from 0 to 1279, each once
- active: int32 [1280], replicated, may hold values from 5 to 640, as said below
Outputs:
- grid: bfloat16 [1280, 4, 2560], P(('wide', 'lev'))
- spec_out: float32 [320, 2, 4, 641], P('wide', None, 'lev')
Inputs may be any that keep to these rules, and one draw needn't show every extreme that they name: `wave_order`: A permutation in which slots 2p and 2p + 1 hold wavenumbers m and 639 - m. `lat_order`: each latitude once. `active`: equals 640 at some latitudes of every draw.
All inputs are finite; a program needn't handle non-finite values.
Results may differ from a plain program's by a relative error of at most 0.0072.
Values may be sent and summed in bfloat16 or wider, within the bound.
No kernel may reach another device: no remote copies, remote signals or barrier semaphores. Data moves between devices by JAX's collectives and lax.ppermute only.
A program may use at most 64 MiB of HBM per device.

v0:
```python
import math

import jax
import jax.numpy as jnp
from jax import lax
from jax.sharding import PartitionSpec as P


def make_basis(wave_order, live_count, points):
    cell_count = 4 * live_count
    cell_float = cell_count.astype(jnp.float32)
    outer_count = points // 128
    outer_ids = jnp.arange(outer_count, dtype=jnp.int32) * 128
    inner_ids = jnp.arange(128, dtype=jnp.int32)
    outer_phase = wave_order[:, None] * outer_ids[None, :] % cell_count
    inner_phase = wave_order[:, None] * inner_ids[None, :] % cell_count
    outer_angle = outer_phase.astype(jnp.float32) * (2.0 * math.pi) / cell_float
    inner_angle = inner_phase.astype(jnp.float32) * (2.0 * math.pi) / cell_float
    cos_outer = jnp.cos(outer_angle)[:, :, None]
    sin_outer = jnp.sin(outer_angle)[:, :, None]
    cos_inner = jnp.cos(inner_angle)[:, None, :]
    sin_inner = jnp.sin(inner_angle)[:, None, :]
    wave_total = wave_order.shape[0]
    cosine = (cos_outer * cos_inner - sin_outer * sin_inner).reshape(wave_total, points)
    sines = (-(sin_outer * cos_inner + cos_outer * sin_inner)).reshape(wave_total, points)
    columns = jnp.arange(points, dtype=jnp.int32)
    alive = (wave_order[:, None] < live_count) & (columns[None, :] < cell_count)
    cosine = jnp.where(alive, cosine, jnp.zeros_like(cosine))
    sines = jnp.where(alive, sines, jnp.zeros_like(sines))
    return jnp.concatenate([cosine, sines], 0).astype(jnp.bfloat16)


def legendre_direct(lat_rows, legendre, owned):
    lat_total, level_depth, parts, slot_count = lat_rows.shape
    unpacked = lat_rows.reshape(lat_total, level_depth, parts, slot_count // 2, 2)
    results = jnp.einsum("qlrps,pcq->psrlc", unpacked, legendre, preferred_element_type=jnp.float32)
    return jnp.where(owned[:, None, None, :], results[:, 0], results[:, 1])


def shards(spec_in, legendre, wind, lat_weight, wave_order, lat_order, active):
    wide_count = lax.axis_size("wide")
    lev_count = lax.axis_size("lev")
    wide_pos = lax.axis_index("wide")
    lev_pos = lax.axis_index("lev")
    pairs_here, coef_count, lat_total = legendre.shape
    wave_total = coef_count - 1
    lat_here, levels, points = wind.shape
    level_depth = spec_in.shape[2]
    local_waves = lax.dynamic_slice_in_dim(wave_order, wide_pos * 2 * pairs_here, 2 * pairs_here)
    owned = (
        jnp.arange(coef_count, dtype=jnp.int32)[None, :] < (wave_total - local_waves[0::2])[:, None]
    )
    keep_mask = owned[:, None, None, :]
    nothing = jnp.zeros_like(spec_in)
    stacked = jnp.stack(
        [jnp.where(keep_mask, spec_in, nothing), jnp.where(keep_mask, nothing, spec_in)], 1
    )
    fourier = jnp.einsum(
        "psrlc,pcq->psrlq", stacked, legendre, preferred_element_type=jnp.float32
    ).astype(jnp.bfloat16)
    ordered = jnp.take(fourier, lat_order, axis=4)
    outgoing = jnp.transpose(ordered, (4, 3, 2, 0, 1)).reshape(
        lat_total, level_depth, 2, 2 * pairs_here
    )
    arrived = lax.all_to_all(
        lax.all_to_all(outgoing, "wide", split_axis=0, concat_axis=3, tiled=True),
        "lev",
        split_axis=0,
        concat_axis=1,
        tiled=True,
    )
    first_slot = (wide_pos * lev_count + lev_pos) * lat_here
    latitudes = lax.dynamic_slice_in_dim(lat_order, first_slot, lat_here)
    counts = jnp.take(active, latitudes)
    weights = jnp.take(lat_weight, latitudes)
    factors = jnp.where(wave_order == 0, 1.0, 2.0).astype(jnp.bfloat16)

    def per_lat(inputs):
        coeffs, wind_rows, live_count, weight = inputs
        basis_rows = make_basis(wave_order, live_count, points)
        scaled = (coeffs * factors).reshape(levels, 2 * wave_total)
        grid_rows = jnp.dot(scaled, basis_rows, preferred_element_type=jnp.float32).astype(
            jnp.bfloat16
        )
        product = (grid_rows.astype(jnp.float32) * wind_rows.astype(jnp.float32)).astype(
            jnp.bfloat16
        )
        folded = lax.dot_general(
            product, basis_rows, (((1,), (1,)), ((), ())), preferred_element_type=jnp.float32
        )
        folded = (folded * (weight / (4 * live_count).astype(jnp.float32))).astype(jnp.bfloat16)
        return (grid_rows, folded.reshape(levels, 2, wave_total))

    grid, folded = lax.map(per_lat, (arrived, wind, counts, weights))
    row_ids = jnp.arange(lat_total, dtype=jnp.int32)
    received = lax.all_to_all(
        lax.all_to_all(folded, "wide", split_axis=3, concat_axis=0, tiled=True),
        "lev",
        split_axis=1,
        concat_axis=0,
        tiled=True,
    )
    lev_src = row_ids // (wide_count * lat_here)
    wide_src = row_ids // lat_here % wide_count
    within = row_ids % lat_here
    slot_index = (wide_src * lev_count + lev_src) * lat_here + within
    position = jnp.zeros((lat_total,), jnp.int32).at[jnp.take(lat_order, slot_index)].set(row_ids)
    spec_out = legendre_direct(jnp.take(received, position, axis=0), legendre, owned)
    return (grid, spec_out)


def solution(mesh):
    in_specs = (
        P("wide", None, "lev", None),
        P("wide", None, None),
        P(("wide", "lev"), None, None),
        P(),
        P(),
        P(),
        P(),
    )
    out_specs = (P(("wide", "lev"), None, None), P("wide", None, "lev", None))
    return jax.shard_map(shards, mesh=mesh, in_specs=in_specs, out_specs=out_specs, check_vma=False)
```

profile of v0, /device:TPU:1, one launch (start us, length us, event | category | flops | bytes accessed | tf_op | source)
XLA Modules:
  0.0 220.1 jit_solution(6892341236998387838)
XLA Ops:
  3.8 4.6 %fusion.38 = bf16[5,2,2,1280]{3,2,1,0:T(2,128)(2,1)S(1)} fusion(bf16[5,641,1280]{2,1,0:T(8,128)(2,1)} %param.10, bf16[5,1,2,1,641]{4,2,1,0,3:T(2,128)(2,1)S(1)} %get-tuple-element.127, bf16[5,1,2,1,641]{4,2,1,0,3:T(2,128)(2,1)S(1)} %get-tuple-element.126), kind=kOutput, calls=%fused_computation.60 | convolution fusion | flops 32896080 | bytes 8281640 | tf_op jit(solution)/shard_map/psrlc,pcq->psrlq/dot_general | solution.py:58
  9.5 4.9 %gather_fusion = bf16[1280,5,2,2]{1,3,2,0:T(2,128)(2,1)S(1)} fusion(bf16[5,2,2,1280]{0,2,3,1:T(2,128)(2,1)S(1)} %copy.62, s32[2048]{0:T(1024)S(1)} %pad_clamp_fusion.2), kind=kCustom, calls=%fused_computation | custom fusion | bytes 107520 | tf_op jit(solution)/shard_map/jit(_take)/gather | solution.py:61
  14.4 4.7 %fusion.41 = bf16[1280,1,2,5,2]{3,2,4,0,1:T(2,128)(2,1)S(1)} fusion(bf16[1280,5,2,2]{1,3,2,0:T(2,128)(2,1)S(1)} %gather_fusion, pred[1280]{0:T(1024)(128)(4,1)S(1)} %compare_and_fusion.1), kind=kLoop, calls=%fused_computation.61 | loop fusion | flops 25600 | bytes 103680 | tf_op jit(solution)/shard_map/transpose | solution.py:62
  22.5 13.2 %all-to-all-start = ((bf16[64,2,200]{2,1,0:T(2,128)(2,1)}), bf16[64,2,200]{2,1,0:T(2,128)(2,1)S(1)}, u32[]{:S(2)}, u32[]{:S(2)}) async-start(bf16[64,2,200]{2,1,0:T(2,128)(2,1)} %reshape.446), calls=%async_computation | async-start | bytes 131072 | tf_op jit(solution)/shard_map/all_to_all | solution.py:66
  35.9 7.1 %gather_fusion.3 = s32[1280]{0:T(1024)S(1)} fusion(s32[1280]{0:T(1024)S(1)} %copy-done.1, s32[2048]{0:T(1024)S(1)} %pad_clamp_fusion.1), kind=kCustom, calls=%fused_computation.3 | custom fusion | bytes 15360 | tf_op jit(solution)/shard_map/jit(_take)/gather | solution.py:107
  43.1 5.2 %scatter_custom_fusion = s32[1280]{0:T(1024)S(1)} fusion(s32[1280]{0:T(1024)S(1)} %fusion.53, s32[1280]{0:T(1024)S(1)} %iota.38, s32[]{:T(128)} %constant.119.clone.1), kind=kCustom, calls=%fused_computation.105 | custom fusion | bytes 5124 | tf_op jit(solution)/shard_map/scatter | solution.py:107
  52.6 4.0 %all-to-all-start.1 = ((bf16[20,1,2,640]{3,2,1,0:T(2,128)(2,1)}), bf16[20,1,2,640]{3,2,1,0:T(2,128)(2,1)S(1)}, u32[]{:S(2)}, u32[]{:S(2)}) async-start(bf16[20,1,2,640]{3,2,1,0:T(2,128)(2,1)} %copy.67), calls=%async_computation.1 | async-start | bytes 102400 | tf_op jit(solution)/shard_map/all_to_all | solution.py:65
  56.7 4.3 %all-to-all-done.1 = bf16[20,1,2,640]{3,2,1,0:T(2,128)(2,1)S(1)} async-done(((bf16[20,1,2,640]{3,2,1,0:T(2,128)(2,1)}), bf16[20,1,2,640]{3,2,1,0:T(2,128)(2,1)S(1)}, u32[]{:S(2)}, u32[]{:S(2)}) %all-to-all-start.1) | async-done | bytes 51232 | tf_op jit(solution)/shard_map/all_to_all | solution.py:65
  61.0 105.5 %while.12 = (s32[]{:T(128)}, bf16[5,4,2560]{2,1,0:T(4,128)(2,1)S(1)}, bf16[5,4,2,640]{3,2,1,0:T(2,128)(2,1)S(1)}, bf16[5,4,2,640]{3,2,0,1:T(2,128)(2,1)S(1)}, bf...) while((s32[]{:T(128)}, ...), condition=%wide.region_1.2_spmd, body=%wide.region_0.1_spmd.sunk | while | flops 99431064 | bytes 34495892 | solution.py:94
  62.2 4.4 %fusion.67 = (f32[640,128]{0,1:T(8,128)S(1)}, f32[640,128]{0,1:T(8,128)S(1)}) fusion(f32[]{:T(128)S(6)} %convert_element_type.93, pred[]{:T(512)S(6)} %lt.253, s32[]{:T(128)S(6)} %select_n.357, s32[640]{0:T(1024)S(1)} %get-tuple-element.233), kind=kLoop, calls=%fused_computation.28.clone.1 | loop fusion | flops 901120 | bytes 657929 | tf_op jit(solution)/shard_map/while/body/eval_jaxpr/cos | solution.py:21
  70.7 3.3 %fusion.69 = (bf16[640,2560]{0,1:T(8,128)(2,1)S(1)}, bf16[640,2560]{0,1:T(8,128)(2,1)}) fusion(bf16[640,20,128]{0,2,1:T(8,128)(2,1)S(1)} %get-tuple-element.197, pred[640]{0:T(1024)(128)(4,1)S(1)} %broadcast_compare_fusion.2, pred[2560]{0:T(1024)(128)(4,1)S(1)} %iota_compare_fusion.3, bf16[640,20,128]{0,2,1:T(8,128)(2,1)S(1)} %get-tuple-element.198), kind=kLoop, calls=%fused_computation.8.clone.1 | loop fusion | flops 4915200 | bytes 13110400 | tf_op jit(solution)/shard_map/convert.1
  74.0 3.9 %bitcast_dynamic-update-slice_fusion.2 = (bf16[5,4,2560]{2,1,0:T(4,128)(2,1)S(1)}, bf16[4,2560]{1,0:T(4,128)(2,1)}) fusion(bf16[5,4,2560]{2,1,0:T(4,128)(2,1)S(1)} %get-tuple-element.216, s32[]{:T(128)} %get-tuple-element.215, bf16[640,2560]{0,1:T(8,128)(2,1)} %get-tuple-element.199, bf16[640,2560]{0,1:T(8,128)(2,1)S(1)} %get-tuple-element.200, ...), kind=kOutput, calls=%fused_computation.43.clone.1 | convolution fusion | flops 39352320 | bytes 6608900 | tf_op jit(solution)/shard_map/while/body/eval_jaxpr/dot_general | solution.py:82
  79.1 2.9 %fusion.70 = bf16[4,1280]{1,0:T(4,128)(2,1)S(1)} fusion(bf16[640,2560]{0,1:T(8,128)(2,1)} %get-tuple-element.199, bf16[640,2560]{0,1:T(8,128)(2,1)S(1)} %get-tuple-element.200, bf16[4,2560]{1,0:T(4,128)(2,1)} %get-tuple-element.202, bf16[5,4,2560]{2,1,0:T(4,128)(2,1)} %get-tuple-element.234, s32[]{:T(128)} %get-tuple-element.215, f32[]{:T(128)S(6)} %div.124), kind=kOutput, calls=%fused_computation.17.clone.1 | convolution fusion | flops 39372800 | bytes 6605316 | tf_op jit(solution)/shard_map/while/body/eval_jaxpr/dot_general | solution.py:88
  83.3 4.4 %fusion.67 = (f32[640,128]{0,1:T(8,128)S(1)}, f32[640,128]{0,1:T(8,128)S(1)}) fusion(f32[]{:T(128)S(6)} %convert_element_type.93, pred[]{:T(512)S(6)} %lt.253, s32[]{:T(128)S(6)} %select_n.357, s32[640]{0:T(1024)S(1)} %get-tuple-element.233), kind=kLoop, calls=%fused_computation.28.clone.1 | loop fusion | flops 901120 | bytes 657929 | tf_op jit(solution)/shard_map/while/body/eval_jaxpr/cos | solution.py:21
  91.8 3.3 %fusion.69 = (bf16[640,2560]{0,1:T(8,128)(2,1)S(1)}, bf16[640,2560]{0,1:T(8,128)(2,1)}) fusion(bf16[640,20,128]{0,2,1:T(8,128)(2,1)S(1)} %get-tuple-element.197, pred[640]{0:T(1024)(128)(4,1)S(1)} %broadcast_compare_fusion.2, pred[2560]{0:T(1024)(128)(4,1)S(1)} %iota_compare_fusion.3, bf16[640,20,128]{0,2,1:T(8,128)(2,1)S(1)} %get-tuple-element.198), kind=kLoop, calls=%fused_computation.8.clone.1 | loop fusion | flops 4915200 | bytes 13110400 | tf_op jit(solution)/shard_map/convert.1
  95.1 3.9 %bitcast_dynamic-update-slice_fusion.2 = (bf16[5,4,2560]{2,1,0:T(4,128)(2,1)S(1)}, bf16[4,2560]{1,0:T(4,128)(2,1)}) fusion(bf16[5,4,2560]{2,1,0:T(4,128)(2,1)S(1)} %get-tuple-element.216, s32[]{:T(128)} %get-tuple-element.215, bf16[640,2560]{0,1:T(8,128)(2,1)} %get-tuple-element.199, bf16[640,2560]{0,1:T(8,128)(2,1)S(1)} %get-tuple-element.200, ...), kind=kOutput, calls=%fused_computation.43.clone.1 | convolution fusion | flops 39352320 | bytes 6608900 | tf_op jit(solution)/shard_map/while/body/eval_jaxpr/dot_general | solution.py:82
  104.4 4.4 %fusion.67 = (f32[640,128]{0,1:T(8,128)S(1)}, f32[640,128]{0,1:T(8,128)S(1)}) fusion(f32[]{:T(128)S(6)} %convert_element_type.93, pred[]{:T(512)S(6)} %lt.253, s32[]{:T(128)S(6)} %select_n.357, s32[640]{0:T(1024)S(1)} %get-tuple-element.233), kind=kLoop, calls=%fused_computation.28.clone.1 | loop fusion | flops 901120 | bytes 657929 | tf_op jit(solution)/shard_map/while/body/eval_jaxpr/cos | solution.py:21
  112.9 3.3 %fusion.69 = (bf16[640,2560]{0,1:T(8,128)(2,1)S(1)}, bf16[640,2560]{0,1:T(8,128)(2,1)}) fusion(bf16[640,20,128]{0,2,1:T(8,128)(2,1)S(1)} %get-tuple-element.197, pred[640]{0:T(1024)(128)(4,1)S(1)} %broadcast_compare_fusion.2, pred[2560]{0:T(1024)(128)(4,1)S(1)} %iota_compare_fusion.3, bf16[640,20,128]{0,2,1:T(8,128)(2,1)S(1)} %get-tuple-element.198), kind=kLoop, calls=%fused_computation.8.clone.1 | loop fusion | flops 4915200 | bytes 13110400 | tf_op jit(solution)/shard_map/convert.1
  116.2 3.9 %bitcast_dynamic-update-slice_fusion.2 = (bf16[5,4,2560]{2,1,0:T(4,128)(2,1)S(1)}, bf16[4,2560]{1,0:T(4,128)(2,1)}) fusion(bf16[5,4,2560]{2,1,0:T(4,128)(2,1)S(1)} %get-tuple-element.216, s32[]{:T(128)} %get-tuple-element.215, bf16[640,2560]{0,1:T(8,128)(2,1)} %get-tuple-element.199, bf16[640,2560]{0,1:T(8,128)(2,1)S(1)} %get-tuple-element.200, ...), kind=kOutput, calls=%fused_computation.43.clone.1 | convolution fusion | flops 39352320 | bytes 6608900 | tf_op jit(solution)/shard_map/while/body/eval_jaxpr/dot_general | solution.py:82
  125.5 4.4 %fusion.67 = (f32[640,128]{0,1:T(8,128)S(1)}, f32[640,128]{0,1:T(8,128)S(1)}) fusion(f32[]{:T(128)S(6)} %convert_element_type.93, pred[]{:T(512)S(6)} %lt.253, s32[]{:T(128)S(6)} %select_n.357, s32[640]{0:T(1024)S(1)} %get-tuple-element.233), kind=kLoop, calls=%fused_computation.28.clone.1 | loop fusion | flops 901120 | bytes 657929 | tf_op jit(solution)/shard_map/while/body/eval_jaxpr/cos | solution.py:21
  134.0 3.3 %fusion.69 = (bf16[640,2560]{0,1:T(8,128)(2,1)S(1)}, bf16[640,2560]{0,1:T(8,128)(2,1)}) fusion(bf16[640,20,128]{0,2,1:T(8,128)(2,1)S(1)} %get-tuple-element.197, pred[640]{0:T(1024)(128)(4,1)S(1)} %broadcast_compare_fusion.2, pred[2560]{0:T(1024)(128)(4,1)S(1)} %iota_compare_fusion.3, bf16[640,20,128]{0,2,1:T(8,128)(2,1)S(1)} %get-tuple-element.198), kind=kLoop, calls=%fused_computation.8.clone.1 | loop fusion | flops 4915200 | bytes 13110400 | tf_op jit(solution)/shard_map/convert.1
  137.3 3.9 %bitcast_dynamic-update-slice_fusion.2 = (bf16[5,4,2560]{2,1,0:T(4,128)(2,1)S(1)}, bf16[4,2560]{1,0:T(4,128)(2,1)}) fusion(bf16[5,4,2560]{2,1,0:T(4,128)(2,1)S(1)} %get-tuple-element.216, s32[]{:T(128)} %get-tuple-element.215, bf16[640,2560]{0,1:T(8,128)(2,1)} %get-tuple-element.199, bf16[640,2560]{0,1:T(8,128)(2,1)S(1)} %get-tuple-element.200, ...), kind=kOutput, calls=%fused_computation.43.clone.1 | convolution fusion | flops 39352320 | bytes 6608900 | tf_op jit(solution)/shard_map/while/body/eval_jaxpr/dot_general | solution.py:82
  146.6 4.4 %fusion.67 = (f32[640,128]{0,1:T(8,128)S(1)}, f32[640,128]{0,1:T(8,128)S(1)}) fusion(f32[]{:T(128)S(6)} %convert_element_type.93, pred[]{:T(512)S(6)} %lt.253, s32[]{:T(128)S(6)} %select_n.357, s32[640]{0:T(1024)S(1)} %get-tuple-element.233), kind=kLoop, calls=%fused_computation.28.clone.1 | loop fusion | flops 901120 | bytes 657929 | tf_op jit(solution)/shard_map/while/body/eval_jaxpr/cos | solution.py:21
  155.1 3.3 %fusion.69 = (bf16[640,2560]{0,1:T(8,128)(2,1)S(1)}, bf16[640,2560]{0,1:T(8,128)(2,1)}) fusion(bf16[640,20,128]{0,2,1:T(8,128)(2,1)S(1)} %get-tuple-element.197, pred[640]{0:T(1024)(128)(4,1)S(1)} %broadcast_compare_fusion.2, pred[2560]{0:T(1024)(128)(4,1)S(1)} %iota_compare_fusion.3, bf16[640,20,128]{0,2,1:T(8,128)(2,1)S(1)} %get-tuple-element.198), kind=kLoop, calls=%fused_computation.8.clone.1 | loop fusion | flops 4915200 | bytes 13110400 | tf_op jit(solution)/shard_map/convert.1
  158.4 3.9 %bitcast_dynamic-update-slice_fusion.2 = (bf16[5,4,2560]{2,1,0:T(4,128)(2,1)S(1)}, bf16[4,2560]{1,0:T(4,128)(2,1)}) fusion(bf16[5,4,2560]{2,1,0:T(4,128)(2,1)S(1)} %get-tuple-element.216, s32[]{:T(128)} %get-tuple-element.215, bf16[640,2560]{0,1:T(8,128)(2,1)} %get-tuple-element.199, bf16[640,2560]{0,1:T(8,128)(2,1)S(1)} %get-tuple-element.200, ...), kind=kOutput, calls=%fused_computation.43.clone.1 | convolution fusion | flops 39352320 | bytes 6608900 | tf_op jit(solution)/shard_map/while/body/eval_jaxpr/dot_general | solution.py:82
  170.3 11.7 %all-to-all-start.2 = ((bf16[64,2,200]{2,1,0:T(2,128)(2,1)}), bf16[64,2,200]{2,1,0:T(2,128)(2,1)S(1)}, u32[]{:S(2)}, u32[]{:S(2)}) async-start(bf16[64,2,200]{2,1,0:T(2,128)(2,1)} %reshape.448), calls=%async_computation.2 | async-start | bytes 131072 | tf_op jit(solution)/shard_map/all_to_all | solution.py:97
  182.0 10.1 %all-to-all-done.2 = bf16[64,2,200]{2,1,0:T(2,128)(2,1)S(1)} async-done(((bf16[64,2,200]{2,1,0:T(2,128)(2,1)}), bf16[64,2,200]{2,1,0:T(2,128)(2,1)S(1)}, u32[]{:S(2)}, u32[]{:S(2)}) %all-to-all-start.2) | async-done | bytes 51232 | tf_op jit(solution)/shard_map/all_to_all | solution.py:97
  193.0 5.7 %copy.80 = bf16[5,4,2,64,10]{4,3,2,1,0:T(8,128)(2,1)S(1)} copy(bf16[5,4,2,64,10]{0,1,2,4,3:T(4,128)(2,1)S(1)} %bitcast.99) | data formatting | bytes 102400 | tf_op jit(solution)/shard_map/all_to_all | solution.py:97
  200.6 3.3 %all-to-all-start.3 = ((bf16[320,4,2,10]{0,2,3,1:T(2,128)(2,1)}), bf16[320,4,2,10]{0,2,3,1:T(2,128)(2,1)S(1)}, u32[]{:S(2)}, u32[]{:S(2)}) async-start(bf16[320,4,2,10]{0,2,3,1:T(2,128)(2,1)} %copy.72), calls=%async_computation.3 | async-start | bytes 122880 | tf_op jit(solution)/shard_map/all_to_all | solution.py:96
  203.9 4.4 %all-to-all-done.3 = bf16[320,4,2,10]{0,2,3,1:T(2,128)(2,1)S(1)} async-done(((bf16[320,4,2,10]{0,2,3,1:T(2,128)(2,1)}), bf16[320,4,2,10]{0,2,3,1:T(2,128)(2,1)S(1)}, u32[]{:S(2)}, u32[]{:S(2)}) %all-to-all-start.3) | async-done | bytes 51232 | tf_op jit(solution)/shard_map/all_to_all | solution.py:96
  208.9 4.4 %gather_fusion.4 = bf16[1280,2,10]{2,1,0:T(2,128)(2,1)S(1)} fusion(bf16[1280,2,10]{2,1,0:T(2,128)(2,1)S(1)} %bitcast.100, s32[2048]{0:T(1024)S(1)} %pad_clamp_fusion), kind=kCustom, calls=%fused_computation.4 | custom fusion | bytes 107520 | tf_op jit(solution)/shard_map/jit(_take)/gather | solution.py:108
  213.8 5.6 %fusion.42 = f32[5,2,2,1,641]{4,2,0,3,1:T(2,128)S(1)} fusion(bf16[5,641,1280]{2,1,0:T(8,128)(2,1)} %param.10, bf16[1280,2,5,2]{0,1,3,2:T(2,128)(2,1)S(1)} %bitcast.107, pred[1280]{0:T(1024)(128)(4,1)S(1)} %compare_and_fusion), kind=kOutput, calls=%fused_computation.62 | convolution fusion | flops 32844800 | bytes 8308560 | tf_op jit(solution)/shard_map/qlrps,pcq->psrlc/dot_general | solution.py:36
  (121 shorter events, 58.5 us)
Async XLA Ops:
  0.6 47.7 %copy-start = (f32[1280]{0:T(1024)S(1)}, f32[1280]{0:T(1024)}, u32[]{:S(2)}) copy-start(f32[1280]{0:T(1024)} %param.12) | copy-start | bytes 15364
  3.8 31.9 %copy-start.3 = (s32[640]{0:T(1024)S(1)}, s32[640]{0:T(1024)}, u32[]{:S(2)}) copy-start(s32[640]{0:T(1024)} %param.13) | copy-start | bytes 7684
  3.8 32.0 %copy-start.1 = (s32[1280]{0:T(1024)S(1)}, s32[1280]{0:T(1024)}, u32[]{:S(2)}) copy-start(s32[1280]{0:T(1024)} %param.14) | copy-start | bytes 15364
  19.1 30.0 %copy-start.2 = (s32[1280]{0:T(1024)S(1)}, s32[1280]{0:T(1024)}, u32[]{:S(2)}) copy-start(s32[1280]{0:T(1024)} %param.15) | copy-start | bytes 15364
  22.5 27.2 %all-to-all-start = ((bf16[64,2,200]{2,1,0:T(2,128)(2,1)}), bf16[64,2,200]{2,1,0:T(2,128)(2,1)S(1)}, u32[]{:S(2)}, u32[]{:S(2)}) async-start(bf16[64,2,200]{2,1,0:T(2,128)(2,1)} %reshape.446), calls=%async_computation | async-start | bytes 131072 | tf_op jit(solution)/shard_map/all_to_all | solution.py:66
  52.6 8.4 %all-to-all-start.1 = ((bf16[20,1,2,640]{3,2,1,0:T(2,128)(2,1)}), bf16[20,1,2,640]{3,2,1,0:T(2,128)(2,1)S(1)}, u32[]{:S(2)}, u32[]{:S(2)}) async-start(bf16[20,1,2,640]{3,2,1,0:T(2,128)(2,1)} %copy.67), calls=%async_computation.1 | async-start | bytes 102400 | tf_op jit(solution)/shard_map/all_to_all | solution.py:65
  166.5 52.9 %copy-start.4 = (bf16[5,4,2560]{2,1,0:T(4,128)(2,1)}, bf16[5,4,2560]{2,1,0:T(4,128)(2,1)S(1)}, u32[]{:S(2)}) copy-start(bf16[5,4,2560]{2,1,0:T(4,128)(2,1)S(1)} %get-tuple-element.96) | copy-start | bytes 307204
  170.3 21.8 %all-to-all-start.2 = ((bf16[64,2,200]{2,1,0:T(2,128)(2,1)}), bf16[64,2,200]{2,1,0:T(2,128)(2,1)S(1)}, u32[]{:S(2)}, u32[]{:S(2)}) async-start(bf16[64,2,200]{2,1,0:T(2,128)(2,1)} %reshape.448), calls=%async_computation.2 | async-start | bytes 131072 | tf_op jit(solution)/shard_map/all_to_all | solution.py:97
  200.6 7.7 %all-to-all-start.3 = ((bf16[320,4,2,10]{0,2,3,1:T(2,128)(2,1)}), bf16[320,4,2,10]{0,2,3,1:T(2,128)(2,1)S(1)}, u32[]{:S(2)}, u32[]{:S(2)}) async-start(bf16[320,4,2,10]{0,2,3,1:T(2,128)(2,1)} %copy.72), calls=%async_computation.3 | async-start | bytes 122880 | tf_op jit(solution)/shard_map/all_to_all | solution.py:96
where the time goes:
time: 221 us; the launch traced here: 220 us
  other arithmetic  65.8 us (30%)
  local copies, waits for them, and re-layouts  51.2 us (23%)
  matrix products  44.2 us (20%)
  starting transfers between devices  32.2 us (15%)
  waiting for transfers between devices  18.8 us (9%)
  loops' own time  6.96 us (3%)
    cos x5, other arithmetic, make_basis(): cos_inner = jnp.cos(inner_angle)[:, None, :]  21.8 us
    dot_general x5, matrix products, per_lat(): jnp.dot(scaled, basis_rows, preferred_element_type=jnp.float32)  19.4 us
    another operation x5, other arithmetic  16.4 us
    dot_general x5, matrix products, per_lat(): lax.dot_general(product, basis_rows, (((1,), (1,)), ((), ())), preferred_...  14.6 us
    all_to_all x1, starting transfers between devices, shards(): lax.all_to_all(outgoing, 'wide', split_axis=0, concat_axis=3, tiled=True)  13.2 us
    sub x5, other arithmetic, make_basis(): cos_outer * cos_inner - sin_outer * sin_inner  12.1 us
    all_to_all x1, starting transfers between devices, shards(): lax.all_to_all(folded, 'wide', split_axis=3, concat_axis=0, tiled=True)  11.7 us
    all_to_all x1, waiting for transfers between devices, shards(): lax.all_to_all(folded, 'wide', split_axis=3, concat_axis=0, tiled=True)  10.1 us
  transfers between devices with their start and end apart: 4, of which 3 were waited for; matrix products, arithmetic and copies ran while one was open for 6% of the time, Pallas kernels for 0%

commit v1 on v0

v1 whole, which is shorter than its diff:
```python
import math

import jax
import jax.numpy as jnp
from jax import lax
from jax.experimental import pallas as pl
from jax.experimental.pallas import tpu as pltpu
from jax.sharding import PartitionSpec as P

F32 = jnp.float32
BF16 = jnp.bfloat16
I32 = jnp.int32
NT = (((1,), (1,)), ((), ()))


def iota(shape, axis):
    return lax.broadcasted_iota(I32, shape, axis)


def pick(table_ref, first_row, row_count, index):
    row = index >> 7
    lane = index & 127
    out = jnp.zeros(index.shape, I32)
    for k in range(row_count):
        line = jnp.broadcast_to(table_ref[first_row + k : first_row + k + 1, :], index.shape)
        got = jnp.take_along_axis(line, lane, axis=1, mode="promise_in_bounds")
        out = jnp.where(row == k, got, out)
    return out


def latitude_table(lat_ref, lat_here):
    halves = []
    index = iota((8, 128), 1) * lat_here + jnp.minimum(iota((8, 128), 0), lat_here - 1)
    for h in range(2):
        halves.append(pick(lat_ref, h * lat_here, lat_here, index))
    return jnp.concatenate(halves, 1)


def fill_onehot(onehot_ref, lat_ref, lat_here):
    lat_total = onehot_ref.shape[0]
    table = latitude_table(lat_ref, lat_here)
    for i in range(lat_here):
        for block in range(0, lat_total, 256):
            rows = iota((256, 256), 0) + block
            hit = rows == table[i : i + 1, :]
            onehot_ref[block : block + 256, i * 256 : (i + 1) * 256] = jnp.where(
                hit, 1.0, 0.0
            ).astype(BF16)


def load_legendre(leg_hbm, leg, sems):
    copies = [
        pltpu.make_async_copy(leg_hbm.at[p], leg.at[p], sems.at[p]) for p in range(leg.shape[0])
    ]
    for copy in copies:
        copy.start()
    return copies


def inverse_kernel(wave_ref, spec_ref, lat_ref, leg_hbm, out_ref, leg, onehot, four, stack, sems):
    pairs, coef, lat_total = leg.shape
    lat_here = lat_ref.shape[0] * 128 // 256
    copies = load_legendre(leg_hbm, leg, sems)
    fill_onehot(onehot, lat_ref, lat_here)
    stack[...] = jnp.zeros_like(stack)
    four[...] = jnp.zeros_like(four)
    wide = lax.axis_index("wide")
    column = iota((2, coef), 1)
    for p in range(pairs):
        first = wave_ref[wide * 2 * pairs + 2 * p]
        own = column < coef - 1 - first
        rows = spec_ref[p].astype(F32)
        nothing = jnp.zeros_like(rows)
        left = jnp.concatenate(
            [
                jnp.where(own, rows, nothing),
                jnp.where(own, nothing, rows),
                nothing,
                nothing,
            ],
            0,
        ).astype(BF16)
        copies[p].wait()
        result = jnp.dot(left, leg[p], preferred_element_type=F32)
        for s in range(2):
            for r in range(2):
                row = s * 12 + r * pairs + p
                four[row : row + 1, :] = result[2 * s + r : 2 * s + r + 1, :]
    placed = jnp.dot(four[...].astype(BF16), onehot[...], preferred_element_type=F32)
    for i in range(lat_here):
        for s in range(2):
            stack[s * 64 + i * 12 : s * 64 + i * 12 + 12, :] = placed[
                s * 12 : s * 12 + 12, i * 256 : (i + 1) * 256
            ]
    out_ref[...] = stack[...].T


def direct_kernel(wave_ref, recv_ref, lat_ref, leg_hbm, out_ref, leg, onehot, sems):
    pairs, coef, lat_total = leg.shape
    lat_here = lat_ref.shape[0] * 128 // 256
    copies = load_legendre(leg_hbm, leg, sems)
    fill_onehot(onehot, lat_ref, lat_here)
    wide = lax.axis_index("wide")
    turned = recv_ref[...].T
    pieces = []
    for i in range(lat_here):
        pieces.append(
            jnp.concatenate(
                [turned[i * 12 : i * 12 + 12, :], turned[64 + i * 12 : 64 + i * 12 + 12, :]], 0
            )
        )
    slots = jnp.concatenate(pieces, 1).astype(BF16)
    ordered = lax.dot_general(slots, onehot[...], NT, preferred_element_type=F32)
    column = iota((1, coef), 1)
    for p in range(pairs):
        first = wave_ref[wide * 2 * pairs + 2 * p]
        own = column < coef - 1 - first
        left = jnp.concatenate(
            [
                ordered[s * 12 + r * pairs + p : s * 12 + r * pairs + p + 1, :]
                for s in range(2)
                for r in range(2)
            ]
            + [jnp.zeros((4, lat_total), F32)],
            0,
        ).astype(BF16)
        copies[p].wait()
        result = lax.dot_general(left, leg[p], NT, preferred_element_type=F32)
        for r in range(2):
            out_ref[p, r, :, :] = jnp.where(own, result[r : r + 1, :], result[2 + r : 3 + r, :])


def turn(x):
    half = x * math.pi
    sq = half * half
    sine = -1.0 / 39916800
    for c in (1.0 / 362880, -1.0 / 5040, 1.0 / 120, -1.0 / 6, 1.0):
        sine = sine * sq + c
    sine = sine * half
    cosine = 1.0 / 479001600
    for c in (-1.0 / 3628800, 1.0 / 40320, -1.0 / 720, 1.0 / 24, -0.5, 1.0):
        cosine = cosine * sq + c
    return 1.0 - 2.0 * sine * sine, 2.0 * sine * cosine


def fill_perm(perm):
    for block in range(0, 512, 256):
        row = iota((256, 512), 0)
        target = (row & 3) * 128 + (block // 256) * 64 + (row >> 2)
        hit = target == iota((256, 512), 1)
        perm[block : block + 256, :] = jnp.where(hit, 1.0, 0.0).astype(BF16)


def fourier_kernel(
    lato_ref, active_ref, weight_ref, recv_ref, wave_ref, wind_ref,
    grid_ref, out_ref,
    perm, four, table, left, backs,
):
    lat_here, levels, points = wind_ref.shape
    blocks = wave_ref.shape[0]
    half = blocks * 128
    outer = points // 128
    fill_perm(perm)
    turned = recv_ref[...].T.astype(BF16)
    joined = jnp.concatenate([turned[:64, :], turned[64:, :]], 1)
    spread = jnp.dot(joined, perm[...], preferred_element_type=F32)
    for l in range(4):
        for copy in range(2):
            four[pl.ds(copy * 4 + l, 64, stride=8), :] = spread[:, l * 128 : (l + 1) * 128]
    backs[...] = jnp.zeros_like(backs)

    lane = iota((8, 128), 1)
    row = iota((8, 128), 0)
    index = (lane & 63) * (2 * blocks) + 2 * jnp.minimum(row, blocks - 1) + (lane >> 6)
    waves = pick(wave_ref, 0, blocks, index)
    waves_f = waves.astype(F32)
    steps_low = row.astype(F32)
    steps_high = jnp.where(row == 0, 8.0, jnp.where(row == 1, 128.0, 256.0))
    upper = row < 4
    first_slot = (lax.axis_index("wide") * lax.axis_size("lev") + lax.axis_index("lev")) * lat_here
    outer_row = iota((outer * 4, 128), 0) >> 2
    point = outer_row * 128 + iota((outer * 4, 128), 1)

    for i in range(lat_here):
        lat = lato_ref[first_slot + i]
        live = jnp.full((8, 128), active_ref[lat], I32)
        cells = (live * 4).astype(F32)
        inverse = 1.0 / cells
        gain = jnp.full((8, 128), weight_ref[lat], F32) / cells
        keep = []
        for p in range(blocks):
            wave = jnp.broadcast_to(waves_f[p : p + 1, :], (8, 128))
            alive = jnp.broadcast_to(waves[p : p + 1, :], (8, 128)) < live
            angles = []
            for steps in (steps_low, steps_high):
                phase = wave * steps
                rest = phase - jnp.round(phase * inverse) * cells
                angles.append(turn(rest * inverse))
            (cos_b, sin_b), (cos_h, sin_h) = angles
            cos8 = jnp.broadcast_to(cos_h[0:1, :], (8, 128))
            sin8 = jnp.broadcast_to(sin_h[0:1, :], (8, 128))
            cosx = jnp.where(upper, 1.0, jnp.broadcast_to(cos_h[1:2, :], (8, 128)))
            sinx = jnp.where(upper, 0.0, jnp.broadcast_to(sin_h[1:2, :], (8, 128)))
            cos2 = jnp.broadcast_to(cos_h[2:3, :], (8, 128))
            sin2 = jnp.broadcast_to(sin_h[2:3, :], (8, 128))
            keep.append((cosx, sinx, cos2, sin2, alive))
            lo, hi = p * 128, half + p * 128
            held = []
            for b in range(16):
                held.append((cos_b, sin_b))
                if b % 2:
                    at = (b - 1) * 8
                    table[at : at + 16, lo : lo + 128] = jnp.concatenate(
                        [held[b - 1][0], cos_b], 0
                    ).astype(BF16)
                    table[at : at + 16, hi : hi + 128] = jnp.concatenate(
                        [held[b - 1][1], sin_b], 0
                    ).astype(BF16)
                if b < 15:
                    cos_b, sin_b = cos_b * cos8 - sin_b * sin8, sin_b * cos8 + cos_b * sin8
            at = (i * 12 + p) * 8
            real = four[at : at + 8, :]
            at = (i * 12 + blocks + p) * 8
            imag = four[at : at + 8, :]
            scale = jnp.where(alive, jnp.where(wave == 0.0, 1.0, 2.0), 0.0)
            real = real * scale
            imag = imag * scale
            real, imag = real * cosx - imag * sinx, real * sinx + imag * cosx
            held = []
            for a in range(outer // 2):
                held.append((real, imag))
                if a % 2:
                    at = (a - 1) * 8
                    left[at : at + 16, lo : lo + 128] = jnp.concatenate(
                        [held[a - 1][0], real], 0
                    ).astype(BF16)
                    left[at : at + 16, hi : hi + 128] = -jnp.concatenate(
                        [held[a - 1][1], imag], 0
                    ).astype(BF16)
                if a < outer // 2 - 1:
                    real, imag = real * cos2 - imag * sin2, real * sin2 + imag * cos2
        values = lax.dot_general(left[...], table[...], NT, preferred_element_type=F32)
        inside = point < active_ref[lat] * 4
        values = jnp.where(inside, values, 0.0).astype(BF16).astype(F32)
        winds = []
        for a in range(outer):
            grid_ref[i, :, a * 128 : (a + 1) * 128] = values[a * 4 : a * 4 + 4, :].astype(BF16)
            winds.append(wind_ref[i, :, a * 128 : (a + 1) * 128].astype(F32))
        product = (values * jnp.concatenate(winds, 0)).astype(BF16)
        sums = jnp.dot(product, table[...], preferred_element_type=F32)
        for p in range(blocks):
            cosx, sinx, cos2, sin2, alive = keep[p]
            lo, hi = p * 128, half + p * 128
            last = outer * 4 - 8
            real = sums[last : last + 8, lo : lo + 128]
            imag = sums[last : last + 8, hi : hi + 128]
            for at in range(last - 8, -1, -8):
                real, imag = (
                    sums[at : at + 8, lo : lo + 128] + (real * cos2 - imag * sin2),
                    sums[at : at + 8, hi : hi + 128] + (real * sin2 + imag * cos2),
                )
            real, imag = real * cosx - imag * sinx, real * sinx + imag * cosx
            real = real + pltpu.roll(real, 4, 0)
            imag = imag + pltpu.roll(imag, 4, 0)
            both = jnp.where(alive, jnp.where(upper, real, -imag) * gain, 0.0)
            at = (i * 12 + p) * 4
            backs[at : at + 4, :] = both[0:4, :]
            at = (i * 12 + blocks + p) * 4
            backs[at : at + 4, :] = both[4:8, :]

    joined = jnp.concatenate([backs[pl.ds(l, 64, stride=4), :] for l in range(4)], 1)
    spread = lax.dot_general(joined.astype(BF16), perm[...], NT, preferred_element_type=F32)
    out_ref[...] = jnp.concatenate([spread[:, :256], spread[:, 256:]], 0).T


def vmem():
    return pl.BlockSpec(memory_space=pltpu.VMEM)


def smem():
    return pl.BlockSpec(memory_space=pltpu.SMEM)


def exchange(rows):
    count, width = rows.shape
    moved = lax.all_to_all(
        rows.reshape(count, 1, width), ("wide", "lev"), split_axis=0, concat_axis=0, tiled=True
    )
    return moved.reshape(count, width)


def shards(spec_in, legendre, wind, lat_weight, wave_order, lat_order, active):
    pairs, coef, lat_total = legendre.shape
    lat_here, levels, points = wind.shape
    devices = lax.axis_size("wide") * lax.axis_size("lev")
    limit = pltpu.CompilerParams(vmem_limit_bytes=40 * 1024 * 1024)
    lat_rows = lat_order.reshape(lat_total // 128, 128)
    wave_rows = wave_order.reshape(wave_order.shape[0] // 128, 128)
    any_space = pl.BlockSpec(memory_space=pl.ANY)

    outgoing = pl.pallas_call(
        inverse_kernel,
        name="legendre_inverse",
        out_shape=jax.ShapeDtypeStruct((devices, 128), F32),
        in_specs=[smem(), vmem(), vmem(), any_space],
        out_specs=vmem(),
        scratch_shapes=[
            pltpu.VMEM((pairs, coef, lat_total), BF16),
            pltpu.VMEM((lat_total, lat_here * devices), BF16),
            pltpu.VMEM((24, lat_total), F32),
            pltpu.VMEM((128, devices), F32),
            pltpu.SemaphoreType.DMA((pairs,)),
        ],
        compiler_params=limit,
    )(wave_order, spec_in.reshape(pairs, 2, coef), lat_rows, legendre)

    grid, outgoing = pl.pallas_call(
        fourier_kernel,
        name="fourier",
        out_shape=(
            jax.ShapeDtypeStruct(wind.shape, BF16),
            jax.ShapeDtypeStruct((devices, 128), F32),
        ),
        in_specs=[smem(), smem(), smem(), vmem(), vmem(), vmem()],
        out_specs=(vmem(), vmem()),
        scratch_shapes=[
            pltpu.VMEM((512, 512), BF16),
            pltpu.VMEM((512, 128), F32),
            pltpu.VMEM((128, 2 * wave_order.shape[0]), BF16),
            pltpu.VMEM((points // 32, 2 * wave_order.shape[0]), BF16),
            pltpu.VMEM((256, 128), F32),
        ],
        compiler_params=limit,
    )(lat_order, active, lat_weight, exchange(outgoing), wave_rows, wind)

    spec_out = pl.pallas_call(
        direct_kernel,
        name="legendre_direct",
        out_shape=jax.ShapeDtypeStruct((pairs, 2, 1, coef), F32),
        in_specs=[smem(), vmem(), vmem(), any_space],
        out_specs=vmem(),
        scratch_shapes=[
            pltpu.VMEM((pairs, coef, lat_total), BF16),
            pltpu.VMEM((lat_total, lat_here * devices), BF16),
            pltpu.SemaphoreType.DMA((pairs,)),
        ],
        compiler_params=limit,
    )(wave_order, exchange(outgoing), lat_rows, legendre)
    return (grid, spec_out)


def solution(mesh):
    in_specs = (
        P("wide", None, "lev", None),
        P("wide", None, None),
        P(("wide", "lev"), None, None),
        P(),
        P(),
        P(),
        P(),
    )
    out_specs = (P(("wide", "lev"), None, None), P("wide", None, "lev", None))
    return jax.shard_map(shards, mesh=mesh, in_specs=in_specs, out_specs=out_specs, check_vma=False)
```

time: 221 us -> 68.2 us (0.31)
  other arithmetic: 65.8 us -> 0 us
  blocking collectives: 0 us -> 46.5 us
  local copies, waits for them, and re-layouts: 51.2 us -> 5.46 us
  matrix products: 44.2 us -> 0 us
  starting transfers between devices: 32.2 us -> 0 us
  waiting for transfers between devices: 18.8 us -> 0 us
  Pallas kernels: 0 us -> 15.3 us
  loops' own time: 6.96 us -> 0 us
    all_to_all x0 -> x2, blocking collectives: none -> 46.5 us  [exchange(): lax.all_to_all(rows.reshape(count, 1, width), ('wide', 'lev'), split_axis...]
    dot_general x12 -> x0, matrix products: 44.2 us -> none  [the longest x5 19.4 us: per_lat(): jnp.dot(scaled, basis_rows, preferred_element_type=jnp.float32)]
    all_to_all x4 -> x0, starting transfers between devices: 32.2 us -> none  [the longest x1 13.2 us: shards(): lax.all_to_all(outgoing, 'wide', split_axis=0, concat_axis=3, tiled=True)]
    cos x10 -> x0, other arithmetic: 26.5 us -> none  [the longest x5 21.8 us: make_basis(): cos_inner = jnp.cos(inner_angle)[:, None, :]]
    all_to_all x4 -> x0, waiting for transfers between devices: 18.8 us -> none  [the longest x1 10.1 us: shards(): lax.all_to_all(folded, 'wide', split_axis=3, concat_axis=0, tiled=True)]
    gather x6 -> x0, local copies, waits for them, and re-layouts: 18.1 us -> none  [the longest x1 7.08 us: shards(): jnp.take(lat_order, slot_index)]
    another operation x6 -> x0, other arithmetic: 17.2 us -> none
    pallas_call x0 -> x3, Pallas kernels: none -> 15.3 us  [the longest x1 6.84 us: shards(): pl.pallas_call(direct_kernel, name='legendre_direct', out_shape=jax.Shape...]
  transfers between devices with their start and end apart: 4 -> 0, of which waited for: 3 -> 0; matrix products, arithmetic and copies ran while one was open for 6% -> 0% of each run, Pallas kernels for 0% -> 0%
where the time goes in v1:
time: 68.2 us; the launch traced here: 67.9 us
  blocking collectives  46.5 us (68%)
  Pallas kernels  15.3 us (22%)
  local copies, waits for them, and re-layouts  5.46 us (8%)
    all_to_all x2, blocking collectives, exchange(): lax.all_to_all(rows.reshape(count, 1, width), ('wide', 'lev'), split_axis...  46.5 us
    pallas_call x1, Pallas kernels, shards(): pl.pallas_call(direct_kernel, name='legendre_direct', out_shape=jax.Shape...  6.84 us
    unnamed x18, local copies, waits for them, and re-layouts  5.46 us
    pallas_call x1, Pallas kernels, shards(): pl.pallas_call(inverse_kernel, name='legendre_inverse', out_shape=jax.Sha...  4.67 us
    pallas_call x1, Pallas kernels, shards(): pl.pallas_call(fourier_kernel, name='fourier', out_shape=(jax.ShapeDtypeS...  3.77 us

profile of v1, /device:TPU:1, one launch (start us, length us, event | category | flops | bytes accessed | tf_op | source)
XLA Modules:
  0.0 67.9 jit_solution(7216890514899627090)
XLA Ops:
  0.6 0.0 copy-start
  0.6 3.3 %copy-done = bf16[5,641,1280]{2,1,0:T(8,128)(2,1)S(1)} copy-done((bf16[5,641,1280]{2,1,0:T(8,128)(2,1)S(1)}, bf16[5,641,1280]{2,1,0:T(8,128)(2,1)}, u32[]{:S(2)}) %copy-start) | copy-done | bytes 8204824
  4.0 0.0 copy-start.3
  4.0 0.7 %copy-done.3 = s32[1280]{0:T(1024)S(1)} copy-done((s32[1280]{0:T(1024)S(1)}, s32[1280]{0:T(1024)}, u32[]{:S(2)}) %copy-start.3) | copy-done | bytes 5144
  4.7 0.0 copy-start.5
  4.7 0.7 %copy-done.5 = s32[640]{0:T(1024)S(1)} copy-done((s32[640]{0:T(1024)S(1)}, s32[640]{0:T(1024)}, u32[]{:S(2)}) %copy-start.5) | copy-done | bytes 2584
  5.4 0.0 copy-start.6
  5.4 0.7 %copy-done.6 = bf16[5,2,1,641]{3,1,2,0:T(2,128)(2,1)S(1)} copy-done((bf16[5,2,1,641]{3,1,2,0:T(2,128)(2,1)S(1)}, bf16[5,2,1,641]{3,1,2,0:T(2,128)(2,1)}, u32[]{:S(2)}) %copy-start.6) | copy-done | bytes 12844
  6.1 0.0 copy-start.2
  6.1 0.0 copy-start.4
  6.1 0.0 copy-start.7
  6.1 0.0 copy-start.8
  6.1 0.0 copy-start.1
  6.1 4.7 %legendre_inverse.1 = f32[256,128]{1,0:T(8,128)S(1)} custom-call(s32[640]{0:T(1024)S(1)} %copy-done.5, bf16[5,2,641]{2,1,0:T(2,128)(2,1)S(1)} %bitcast.18, s32[10,128]{1,0:T(8,128)S(1)} %bitcast.15, bf16[5,641,1280]{2,1,0:T(8,128)(2,1)S(1)} %copy-done), custom_call_target="tpu_custom_call" | custom-call | tf_op jit(solution)/shard_map/legendre_inverse/pallas_call | solution.py:301
  10.8 28.3 %all_to_all.10 = f32[256,1,128]{2,1,0:T(1,128)S(1)} all-to-all(f32[256,1,128]{2,1,0:T(1,128)S(1)} %bitcast.12), channel_id=1, replica_groups=mesh['wide'=64,'lev'=4] {'wide','lev'}, dimensions={0} | all-to-all | bytes 262144 | tf_op jit(solution)/shard_map/all_to_all | solution.py:286
  39.0 0.0 copy-done.2
  39.0 0.0 copy-done.4
  39.0 0.0 copy-done.7
  39.0 0.0 copy-done.8
  39.1 3.8 %fourier.1 = (bf16[5,4,2560]{2,1,0:T(4,128)(2,1)}, f32[256,128]{1,0:T(8,128)S(1)}) custom-call(s32[1280]{0:T(1024)S(1)} %copy-done.4, s32[1280]{0:T(1024)S(1)} %copy-done.7, f32[1280]{0:T(1024)S(1)} %copy-done.8, f32[256,128]{1,0:T(8,128)S(1)} %bitcast.13, s32[5,128]{1,0:T(8,128)S(1)} %bitcast.17, bf16[5,4,2560]{2,1,0:T(4,128)(2,1)S(1)} %copy-done.2), custom_call_target="tpu_custom_call" | custom-call | tf_op jit(solution)/shard_map/fourier/pallas_call | solution.py:317
  42.8 18.2 %all_to_all.11 = f32[256,1,128]{2,1,0:T(1,128)S(1)} all-to-all(f32[256,1,128]{2,1,0:T(1,128)S(1)} %bitcast.14), channel_id=1, replica_groups=mesh['wide'=64,'lev'=4] {'wide','lev'}, dimensions={0} | all-to-all | bytes 262144 | tf_op jit(solution)/shard_map/all_to_all | solution.py:286
  61.1 0.0 copy-done.1
  61.1 6.8 %legendre_direct.1 = f32[5,2,1,641]{3,2,1,0:T(1,128)} custom-call(s32[640]{0:T(1024)S(1)} %copy-done.5, f32[256,128]{1,0:T(8,128)S(1)} %bitcast.11, s32[10,128]{1,0:T(8,128)S(1)} %bitcast.16, bf16[5,641,1280]{2,1,0:T(8,128)(2,1)S(1)} %copy-done.1), custom_call_target="tpu_custom_call" | custom-call | tf_op jit(solution)/shard_map/legendre_direct/pallas_call | solution.py:336
Async XLA Ops:
  0.6 3.4 %copy-start = (bf16[5,641,1280]{2,1,0:T(8,128)(2,1)S(1)}, bf16[5,641,1280]{2,1,0:T(8,128)(2,1)}, u32[]{:S(2)}) copy-start(bf16[5,641,1280]{2,1,0:T(8,128)(2,1)} %leg_hbm.3) | copy-start | bytes 24614404
  4.0 0.7 %copy-start.3 = (s32[1280]{0:T(1024)S(1)}, s32[1280]{0:T(1024)}, u32[]{:S(2)}) copy-start(s32[1280]{0:T(1024)} %lato_ref.1) | copy-start | bytes 15364
  4.7 0.7 %copy-start.5 = (s32[640]{0:T(1024)S(1)}, s32[640]{0:T(1024)}, u32[]{:S(2)}) copy-start(s32[640]{0:T(1024)} %wave_ref.3) | copy-start | bytes 7684
  5.4 0.7 %copy-start.6 = (bf16[5,2,1,641]{3,1,2,0:T(2,128)(2,1)S(1)}, bf16[5,2,1,641]{3,1,2,0:T(2,128)(2,1)}, u32[]{:S(2)}) copy-start(bf16[5,2,1,641]{3,1,2,0:T(2,128)(2,1)} %param.7) | copy-start | bytes 38464
  6.1 32.9 %copy-start.2 = (bf16[5,4,2560]{2,1,0:T(4,128)(2,1)S(1)}, bf16[5,4,2560]{2,1,0:T(4,128)(2,1)}, u32[]{:S(2)}) copy-start(bf16[5,4,2560]{2,1,0:T(4,128)(2,1)} %wind_ref.1) | copy-start | bytes 307204
  6.1 32.9 %copy-start.4 = (s32[1280]{0:T(1024)S(1)}, s32[1280]{0:T(1024)}, u32[]{:S(2)}) copy-start(s32[1280]{0:T(1024)} %lato_ref.1) | copy-start | bytes 15364
  6.1 33.0 %copy-start.7 = (s32[1280]{0:T(1024)S(1)}, s32[1280]{0:T(1024)}, u32[]{:S(2)}) copy-start(s32[1280]{0:T(1024)} %active_ref.1) | copy-start | bytes 15364
  6.1 33.0 %copy-start.8 = (f32[1280]{0:T(1024)S(1)}, f32[1280]{0:T(1024)}, u32[]{:S(2)}) copy-start(f32[1280]{0:T(1024)} %weight_ref.1) | copy-start | bytes 15364
  6.1 55.0 %copy-start.1 = (bf16[5,641,1280]{2,1,0:T(8,128)(2,1)S(1)}, bf16[5,641,1280]{2,1,0:T(8,128)(2,1)}, u32[]{:S(2)}) copy-start(bf16[5,641,1280]{2,1,0:T(8,128)(2,1)} %leg_hbm.3) | copy-start | bytes 24614404

commit v2 on v1

v2 whole, which is shorter than its diff:
```python
import math

import jax
import jax.numpy as jnp
from jax import lax
from jax.experimental import pallas as pl
from jax.experimental.pallas import tpu as pltpu
from jax.sharding import PartitionSpec as P

F32 = jnp.float32
BF16 = jnp.bfloat16
I32 = jnp.int32
NT = (((1,), (1,)), ((), ()))


def iota(shape, axis):
    return lax.broadcasted_iota(I32, shape, axis)


def pick(table_ref, first_row, row_count, index):
    row = index >> 7
    lane = index & 127
    out = jnp.zeros(index.shape, I32)
    for k in range(row_count):
        line = jnp.broadcast_to(table_ref[first_row + k : first_row + k + 1, :], index.shape)
        got = jnp.take_along_axis(line, lane, axis=1, mode="promise_in_bounds")
        out = jnp.where(row == k, got, out)
    return out


def latitude_table(lat_ref, lat_here):
    halves = []
    index = iota((8, 128), 1) * lat_here + jnp.minimum(iota((8, 128), 0), lat_here - 1)
    for h in range(2):
        halves.append(pick(lat_ref, h * lat_here, lat_here, index))
    return jnp.concatenate(halves, 1)


def fill_onehot(onehot_ref, lat_ref, lat_here):
    lat_total = onehot_ref.shape[0]
    table = latitude_table(lat_ref, lat_here)
    for i in range(lat_here):
        for block in range(0, lat_total, 256):
            rows = iota((256, 256), 0) + block
            hit = rows == table[i : i + 1, :]
            onehot_ref[block : block + 256, i * 256 : (i + 1) * 256] = jnp.where(
                hit, 1.0, 0.0
            ).astype(BF16)


def turn(x):
    half = x * math.pi
    sq = half * half
    sine = -1.0 / 39916800
    for c in (1.0 / 362880, -1.0 / 5040, 1.0 / 120, -1.0 / 6, 1.0):
        sine = sine * sq + c
    sine = sine * half
    cosine = 1.0 / 479001600
    for c in (-1.0 / 3628800, 1.0 / 40320, -1.0 / 720, 1.0 / 24, -0.5, 1.0):
        cosine = cosine * sq + c
    return 1.0 - 2.0 * sine * sine, 2.0 * sine * cosine


def fill_perm(perm):
    for block in range(0, 512, 256):
        row = iota((256, 512), 0)
        target = (row & 3) * 128 + (block // 256) * 64 + (row >> 2)
        hit = target == iota((256, 512), 1)
        perm[block : block + 256, :] = jnp.where(hit, 1.0, 0.0).astype(BF16)


def wave_table(wave_rows_ref, blocks):
    lane = iota((8, 128), 1)
    row = iota((8, 128), 0)
    index = (lane & 63) * (2 * blocks) + 2 * jnp.minimum(row, blocks - 1) + (lane >> 6)
    return pick(wave_rows_ref, 0, blocks, index)


def fill_tables(table, rotors, wave_rows_ref, lato_ref, active_ref, weight_ref):
    lat_here = table.shape[0]
    blocks = wave_rows_ref.shape[0]
    half = blocks * 128
    row = iota((8, 128), 0)
    waves = wave_table(wave_rows_ref, blocks)
    waves_f = waves.astype(F32)
    steps_low = row.astype(F32)
    steps_high = jnp.where(row == 0, 8.0, jnp.where(row == 1, 128.0, 256.0))
    first_slot = (lax.axis_index("wide") * lax.axis_size("lev") + lax.axis_index("lev")) * lat_here
    for i in range(lat_here):
        lat = lato_ref[first_slot + i]
        live = jnp.full((8, 128), active_ref[lat], I32)
        cells = (live * 4).astype(F32)
        inverse = 1.0 / cells
        gain = jnp.full((8, 128), weight_ref[lat], F32) / cells
        for p in range(blocks):
            wave = jnp.broadcast_to(waves_f[p : p + 1, :], (8, 128))
            alive = jnp.broadcast_to(waves[p : p + 1, :], (8, 128)) < live
            angles = []
            for steps in (steps_low, steps_high):
                phase = wave * steps
                rest = phase - jnp.round(phase * inverse) * cells
                angles.append(turn(rest * inverse))
            (cos_b, sin_b), (cos_h, sin_h) = angles
            cos8 = jnp.broadcast_to(cos_h[0:1, :], (8, 128))
            sin8 = jnp.broadcast_to(sin_h[0:1, :], (8, 128))
            lo, hi = p * 128, half + p * 128
            held = []
            for b in range(16):
                held.append((cos_b, sin_b))
                if b % 2:
                    at = (b - 1) * 8
                    table[i, at : at + 16, lo : lo + 128] = jnp.concatenate(
                        [held[b - 1][0], cos_b], 0
                    ).astype(BF16)
                    table[i, at : at + 16, hi : hi + 128] = jnp.concatenate(
                        [held[b - 1][1], sin_b], 0
                    ).astype(BF16)
                if b < 15:
                    cos_b, sin_b = cos_b * cos8 - sin_b * sin8, sin_b * cos8 + cos_b * sin8
            scale = jnp.where(alive, jnp.where(wave == 0.0, 1.0, 2.0), 0.0)
            lines = (
                cos_h[1:2, :], sin_h[1:2, :], cos_h[2:3, :], sin_h[2:3, :],
                scale[0:1, :], jnp.where(alive, gain, 0.0)[0:1, :], cells[0:1, :],
            )
            at = (i * blocks + p) * 8
            for n, line in enumerate(lines):
                rotors[at + n : at + n + 1, :] = line


def inverse_kernel(
    wave_hbm, wave_rows_hbm, spec_hbm, lat_hbm, lat_rows_hbm, active_hbm, weight_hbm, leg_hbm,
    out_ref, leg, onehot, table, rotors, perm,
    wave_ref, wave_rows_ref, spec_ref, lat_ref, lat_rows_ref, active_ref, weight_ref,
    four, stack, small_sems, sems,
):
    pairs, coef, lat_total = leg.shape
    lat_here = table.shape[0]
    small = [
        pltpu.make_async_copy(source, target, small_sems.at[n])
        for n, (source, target) in enumerate(
            (
                (lat_rows_hbm, lat_rows_ref),
                (wave_rows_hbm, wave_rows_ref),
                (lat_hbm, lat_ref),
                (active_hbm, active_ref),
                (weight_hbm, weight_ref),
                (wave_hbm, wave_ref),
                (spec_hbm, spec_ref),
            )
        )
    ]
    copies = [pltpu.make_async_copy(leg_hbm.at[p], leg.at[p], sems.at[p]) for p in range(pairs)]
    for copy in small + copies:
        copy.start()
    stack[...] = jnp.zeros_like(stack)
    four[...] = jnp.zeros_like(four)
    for copy in small:
        copy.wait()
    fill_onehot(onehot, lat_rows_ref, lat_here)
    fill_tables(table, rotors, wave_rows_ref, lat_ref, active_ref, weight_ref)
    fill_perm(perm)
    wide = lax.axis_index("wide")
    column = iota((2, coef), 1)
    for p in range(pairs):
        first = wave_ref[wide * 2 * pairs + 2 * p]
        own = column < coef - 1 - first
        rows = spec_ref[p].astype(F32)
        nothing = jnp.zeros_like(rows)
        left = jnp.concatenate(
            [
                jnp.where(own, rows, nothing),
                jnp.where(own, nothing, rows),
                nothing,
                nothing,
            ],
            0,
        ).astype(BF16)
        copies[p].wait()
        result = jnp.dot(left, leg[p], preferred_element_type=F32)
        for s in range(2):
            for r in range(2):
                row = s * 12 + r * pairs + p
                four[row : row + 1, :] = result[2 * s + r : 2 * s + r + 1, :]
    placed = jnp.dot(four[...].astype(BF16), onehot[...], preferred_element_type=F32)
    for i in range(lat_here):
        for s in range(2):
            stack[s * 64 + i * 12 : s * 64 + i * 12 + 12, :] = placed[
                s * 12 : s * 12 + 12, i * 256 : (i + 1) * 256
            ]
    out_ref[...] = stack[...].T


def direct_kernel(wave_ref, recv_ref, onehot, leg, out_ref):
    pairs, coef, lat_total = leg.shape
    lat_here = lat_total // 256
    wide = lax.axis_index("wide")
    turned = recv_ref[...].T
    pieces = []
    for i in range(lat_here):
        pieces.append(
            jnp.concatenate(
                [turned[i * 12 : i * 12 + 12, :], turned[64 + i * 12 : 64 + i * 12 + 12, :]], 0
            )
        )
    slots = jnp.concatenate(pieces, 1).astype(BF16)
    ordered = lax.dot_general(slots, onehot[...], NT, preferred_element_type=F32)
    column = iota((1, coef), 1)
    for p in range(pairs):
        first = wave_ref[wide * 2 * pairs + 2 * p]
        own = column < coef - 1 - first
        left = jnp.concatenate(
            [
                ordered[s * 12 + r * pairs + p : s * 12 + r * pairs + p + 1, :]
                for s in range(2)
                for r in range(2)
            ]
            + [jnp.zeros((4, lat_total), F32)],
            0,
        ).astype(BF16)
        result = lax.dot_general(left, leg[p], NT, preferred_element_type=F32)
        for r in range(2):
            out_ref[p, r, :, :] = jnp.where(own, result[r : r + 1, :], result[2 + r : 3 + r, :])


def fourier_kernel(
    recv_ref, table, rotors, perm, wind_ref, grid_ref, out_ref, four, left, backs,
):
    lat_here, levels, points = wind_ref.shape
    half = table.shape[2] // 2
    blocks = half // 128
    outer = points // 128
    turned = recv_ref[...].T.astype(BF16)
    joined = jnp.concatenate([turned[:64, :], turned[64:, :]], 1)
    spread = jnp.dot(joined, perm[...], preferred_element_type=F32)
    for l in range(4):
        for copy in range(2):
            four[pl.ds(copy * 4 + l, 64, stride=8), :] = spread[:, l * 128 : (l + 1) * 128]
    backs[...] = jnp.zeros_like(backs)
    upper = iota((8, 128), 0) < 4
    outer_row = iota((outer * 4, 128), 0) >> 2
    point = (outer_row * 128 + iota((outer * 4, 128), 1)).astype(F32)

    def rotor(i, p, n):
        at = (i * blocks + p) * 8 + n
        return jnp.broadcast_to(rotors[at : at + 1, :], (8, 128))

    for i in range(lat_here):
        for p in range(blocks):
            cosx = jnp.where(upper, 1.0, rotor(i, p, 0))
            sinx = jnp.where(upper, 0.0, rotor(i, p, 1))
            cos2, sin2, scale = (rotor(i, p, n) for n in (2, 3, 4))
            lo, hi = p * 128, half + p * 128
            at = (i * 12 + p) * 8
            real = four[at : at + 8, :] * scale
            at = (i * 12 + blocks + p) * 8
            imag = four[at : at + 8, :] * scale
            real, imag = real * cosx - imag * sinx, real * sinx + imag * cosx
            held = []
            for a in range(outer // 2):
                held.append((real, imag))
                if a % 2:
                    at = (a - 1) * 8
                    left[i, at : at + 16, lo : lo + 128] = jnp.concatenate(
                        [held[a - 1][0], real], 0
                    ).astype(BF16)
                    left[i, at : at + 16, hi : hi + 128] = -jnp.concatenate(
                        [held[a - 1][1], imag], 0
                    ).astype(BF16)
                if a < outer // 2 - 1:
                    real, imag = real * cos2 - imag * sin2, real * sin2 + imag * cos2
        values = lax.dot_general(left[i], table[i], NT, preferred_element_type=F32)
        cells = jnp.broadcast_to(rotors[i * blocks * 8 + 6 : i * blocks * 8 + 7, :], point.shape)
        values = jnp.where(point < cells, values, 0.0).astype(BF16).astype(F32)
        winds = []
        for a in range(outer):
            grid_ref[i, :, a * 128 : (a + 1) * 128] = values[a * 4 : a * 4 + 4, :].astype(BF16)
            winds.append(wind_ref[i, :, a * 128 : (a + 1) * 128].astype(F32))
        product = (values * jnp.concatenate(winds, 0)).astype(BF16)
        sums = jnp.dot(product, table[i], preferred_element_type=F32)
        for p in range(blocks):
            cosx = jnp.where(upper, 1.0, rotor(i, p, 0))
            sinx = jnp.where(upper, 0.0, rotor(i, p, 1))
            cos2, sin2, gain = (rotor(i, p, n) for n in (2, 3, 5))
            lo, hi = p * 128, half + p * 128
            last = outer * 4 - 8
            real = sums[last : last + 8, lo : lo + 128]
            imag = sums[last : last + 8, hi : hi + 128]
            for at in range(last - 8, -1, -8):
                real, imag = (
                    sums[at : at + 8, lo : lo + 128] + (real * cos2 - imag * sin2),
                    sums[at : at + 8, hi : hi + 128] + (real * sin2 + imag * cos2),
                )
            real, imag = real * cosx - imag * sinx, real * sinx + imag * cosx
            real = real + pltpu.roll(real, 4, 0)
            imag = imag + pltpu.roll(imag, 4, 0)
            both = jnp.where(upper, real, -imag) * gain
            at = (i * 12 + p) * 4
            backs[at : at + 4, :] = both[0:4, :]
            at = (i * 12 + blocks + p) * 4
            backs[at : at + 4, :] = both[4:8, :]

    joined = jnp.concatenate([backs[pl.ds(l, 64, stride=4), :] for l in range(4)], 1)
    spread = lax.dot_general(joined.astype(BF16), perm[...], NT, preferred_element_type=F32)
    out_ref[...] = jnp.concatenate([spread[:, :256], spread[:, 256:]], 0).T


def vmem():
    return pl.BlockSpec(memory_space=pltpu.VMEM)


def hbm():
    return pl.BlockSpec(memory_space=pltpu.HBM)


def smem():
    return pl.BlockSpec(memory_space=pltpu.SMEM)


def in_hbm(x):
    return pltpu.with_memory_space_constraint(x, pltpu.HBM)


def exchange(rows):
    count, width = rows.shape
    moved = lax.all_to_all(
        rows.reshape(count, 1, width), ("wide", "lev"), split_axis=0, concat_axis=0, tiled=True
    )
    return moved.reshape(count, width)


def shards(spec_in, legendre, wind, lat_weight, wave_order, lat_order, active):
    pairs, coef, lat_total = legendre.shape
    lat_here, levels, points = wind.shape
    devices = lat_total // lat_here
    limit = pltpu.CompilerParams(vmem_limit_bytes=24 * 1024 * 1024)
    lat_rows = lat_order.reshape(lat_total // 128, 128)
    wave_rows = wave_order.reshape(wave_order.shape[0] // 128, 128)

    waves = wave_order.shape[0]
    operands = (
        wave_order, wave_rows, spec_in.reshape(pairs, 2, coef), lat_order, lat_rows, active,
        lat_weight, legendre,
    )
    outgoing, leg_here, onehot, table, rotors, perm = pl.pallas_call(
        inverse_kernel,
        name="legendre_inverse",
        out_shape=(
            jax.ShapeDtypeStruct((devices, 128), F32),
            jax.ShapeDtypeStruct(legendre.shape, BF16),
            jax.ShapeDtypeStruct((lat_total, lat_total), BF16),
            jax.ShapeDtypeStruct((lat_here, 128, 2 * waves), BF16),
            jax.ShapeDtypeStruct((lat_here * waves // 128 * 8, 128), F32),
            jax.ShapeDtypeStruct((512, 512), BF16),
        ),
        in_specs=[hbm()] * len(operands),
        out_specs=(vmem(),) * 6,
        scratch_shapes=[
            pltpu.SMEM(wave_order.shape, I32),
            pltpu.VMEM(wave_rows.shape, I32),
            pltpu.VMEM((pairs, 2, coef), BF16),
            pltpu.SMEM(lat_order.shape, I32),
            pltpu.VMEM(lat_rows.shape, I32),
            pltpu.SMEM(active.shape, I32),
            pltpu.SMEM(lat_weight.shape, F32),
            pltpu.VMEM((24, lat_total), F32),
            pltpu.VMEM((128, devices), F32),
            pltpu.SemaphoreType.DMA((7,)),
            pltpu.SemaphoreType.DMA((pairs,)),
        ],
        compiler_params=limit,
    )(*(in_hbm(x) for x in operands))

    grid, outgoing = pl.pallas_call(
        fourier_kernel,
        name="fourier",
        out_shape=(
            jax.ShapeDtypeStruct(wind.shape, BF16),
            jax.ShapeDtypeStruct((devices, 128), F32),
        ),
        in_specs=[vmem()] * 5,
        out_specs=(vmem(), vmem()),
        scratch_shapes=[
            pltpu.VMEM((512, 128), F32),
            pltpu.VMEM((lat_here, points // 32, 2 * waves), BF16),
            pltpu.VMEM((256, 128), F32),
        ],
        compiler_params=limit,
    )(exchange(outgoing), table, rotors, perm, wind)

    spec_out = pl.pallas_call(
        direct_kernel,
        name="legendre_direct",
        out_shape=jax.ShapeDtypeStruct((pairs, 2, 1, coef), F32),
        in_specs=[smem(), vmem(), vmem(), vmem()],
        out_specs=vmem(),
        compiler_params=limit,
    )(wave_order, exchange(outgoing), onehot, leg_here)
    return (grid, spec_out)


def solution(mesh):
    in_specs = (
        P("wide", None, "lev", None),
        P("wide", None, None),
        P(("wide", "lev"), None, None),
        P(),
        P(),
        P(),
        P(),
    )
    out_specs = (P(("wide", "lev"), None, None), P("wide", None, "lev", None))
    return jax.shard_map(shards, mesh=mesh, in_specs=in_specs, out_specs=out_specs, check_vma=False)
```

time: 68.2 us -> 61.8 us (0.906)
  local copies, waits for them, and re-layouts: 5.46 us -> 0.01 us
  Pallas kernels: 15.3 us -> 14.5 us
    unnamed x18 -> x4, local copies, waits for them, and re-layouts: 5.46 us -> 0.01 us
    pallas_call x1, Pallas kernels: 4.67 us -> 7.25 us  [shards(): pl.pallas_call(inverse_kernel, name='legendre_inverse', out_shape=(jax.Sh...]
    pallas_call x1, Pallas kernels: 6.84 us -> 4.46 us  [shards(): pl.pallas_call(direct_kernel, name='legendre_direct', out_shape=jax.Shape...]
    pallas_call x1, Pallas kernels: 3.77 us -> 2.8 us  [shards(): pl.pallas_call(fourier_kernel, name='fourier', out_shape=(jax.ShapeDtypeS...]
where the time goes in v2:
time: 61.8 us; the launch traced here: 61.7 us
  blocking collectives  46.5 us (75%)
  Pallas kernels  14.5 us (23%)
  between operations  0.66 us (1%)
    all_to_all x2, blocking collectives, exchange(): lax.all_to_all(rows.reshape(count, 1, width), ('wide', 'lev'), split_axis...  46.5 us
    pallas_call x1, Pallas kernels, shards(): pl.pallas_call(inverse_kernel, name='legendre_inverse', out_shape=(jax.Sh...  7.25 us
    pallas_call x1, Pallas kernels, shards(): pl.pallas_call(direct_kernel, name='legendre_direct', out_shape=jax.Shape...  4.46 us
    pallas_call x1, Pallas kernels, shards(): pl.pallas_call(fourier_kernel, name='fourier', out_shape=(jax.ShapeDtypeS...  2.8 us

profile of v2, /device:TPU:1, one launch (start us, length us, event | category | flops | bytes accessed | tf_op | source)
XLA Modules:
  0.0 61.7 jit_solution(11589131352997091953)
XLA Ops:
  0.6 0.0 copy-start.1
  0.6 0.0 copy-start
  0.7 7.2 %legendre_inverse.1 = (f32[256,128]{1,0:T(8,128)S(1)}, bf16[5,641,1280]{2,1,0:T(8,128)(2,1)S(1)}, bf16[1280,1280]{1,0:T(8,128)(2,1)S(1)}, bf16[5,128,1280]{2,1,0...) custom-call(s32[640]{0:T(1024)} %wave_ref.1, s32[5,128]{1,0:T(8,128)} %bitcast.15, ...), custom_call_target="tpu_custom_call" | custom-call | tf_op jit(solution)/shard_map/legendre_inverse/pallas_call | solution.py:344
  7.9 28.3 %all_to_all.10 = f32[256,1,128]{2,1,0:T(1,128)S(1)} all-to-all(f32[256,1,128]{2,1,0:T(1,128)S(1)} %bitcast.13), channel_id=1, replica_groups=mesh['wide'=64,'lev'=4] {'wide','lev'}, dimensions={0} | all-to-all | bytes 262144 | tf_op jit(solution)/shard_map/all_to_all | solution.py:325
  36.2 0.0 copy-done
  36.2 2.8 %fourier.1 = (bf16[5,4,2560]{2,1,0:T(4,128)(2,1)}, f32[256,128]{1,0:T(8,128)S(1)}) custom-call(f32[256,128]{1,0:T(8,128)S(1)} %bitcast.12, bf16[5,128,1280]{2,1,0:T(8,128)(2,1)S(1)} %get-tuple-element.11.table, f32[200,128]{1,0:T(8,128)S(1)} %get-tuple-element.12.rotors, bf16[512,512]{1,0:T(8,128)(2,1)S(1)} %get-tuple-element.13.perm, ...), custom_call_target="tpu_custom_call" | custom-call | tf_op jit(solution)/shard_map/fourier/pallas_call | solution.py:373
  39.0 18.2 %all_to_all.11 = f32[256,1,128]{2,1,0:T(1,128)S(1)} all-to-all(f32[256,1,128]{2,1,0:T(1,128)S(1)} %bitcast.14), channel_id=1, replica_groups=mesh['wide'=64,'lev'=4] {'wide','lev'}, dimensions={0} | all-to-all | bytes 262144 | tf_op jit(solution)/shard_map/all_to_all | solution.py:325
  57.2 0.0 copy-done.1
  57.2 4.5 %legendre_direct.1 = f32[5,2,1,641]{3,2,1,0:T(1,128)} custom-call(s32[640]{0:T(1024)S(1)} %copy-done.1, f32[256,128]{1,0:T(8,128)S(1)} %bitcast.11, bf16[1280,1280]{1,0:T(8,128)(2,1)S(1)} %get-tuple-element.16.onehot, bf16[5,641,1280]{2,1,0:T(8,128)(2,1)S(1)} %get-tuple-element.17.leg), custom_call_target="tpu_custom_call" | custom-call | tf_op jit(solution)/shard_map/legendre_direct/pallas_call | solution.py:390
Async XLA Ops:
  0.6 56.6 %copy-start.1 = (s32[640]{0:T(1024)S(1)}, s32[640]{0:T(1024)}, u32[]{:S(2)}) copy-start(s32[640]{0:T(1024)} %wave_ref.1) | copy-start | bytes 7684
  0.6 35.5 %copy-start = (bf16[5,4,2560]{2,1,0:T(4,128)(2,1)S(1)}, bf16[5,4,2560]{2,1,0:T(4,128)(2,1)}, u32[]{:S(2)}) copy-start(bf16[5,4,2560]{2,1,0:T(4,128)(2,1)} %wind_ref.1) | copy-start | bytes 307204

commit v3 on v2

--- a/solution.py
+++ b/solution.py
@@ -11,6 +11,7 @@
 BF16 = jnp.bfloat16
 I32 = jnp.int32
 NT = (((1,), (1,)), ((), ()))
+BUSY = pl.CostEstimate(flops=4_000_000_000, bytes_accessed=16_000_000, transcendentals=0)
 
 
 def iota(shape, axis):
@@ -36,16 +37,25 @@
     return jnp.concatenate(halves, 1)
 
 
-def fill_onehot(onehot_ref, lat_ref, lat_here):
-    lat_total = onehot_ref.shape[0]
-    table = latitude_table(lat_ref, lat_here)
-    for i in range(lat_here):
-        for block in range(0, lat_total, 256):
-            rows = iota((256, 256), 0) + block
-            hit = rows == table[i : i + 1, :]
-            onehot_ref[block : block + 256, i * 256 : (i + 1) * 256] = jnp.where(
-                hit, 1.0, 0.0
-            ).astype(BF16)
+def gather_tiles(tiles, index):
+    tile = index >> 7
+    lane = index & 127
+    out = jnp.zeros(index.shape, tiles[0].dtype)
+    for k, source in enumerate(tiles):
+        got = jnp.take_along_axis(source, lane, axis=1, mode="promise_in_bounds")
+        out = jnp.where(tile == k, got, out)
+    return out
+
+
+def start_copies(pairs, sems):
+    copies = [pltpu.make_async_copy(a, b, sems.at[n]) for n, (a, b) in enumerate(pairs)]
+    for copy in copies:
+        copy.start()
+    return copies
+
+
+def group_pairs(group, pairs):
+    return range(2 * group, min(2 * group + 2, pairs))
 
 
 def turn(x):
@@ -128,109 +138,155 @@
 
 
 def inverse_kernel(
-    wave_hbm, wave_rows_hbm, spec_hbm, lat_hbm, lat_rows_hbm, active_hbm, weight_hbm, leg_hbm,
-    out_ref, leg, onehot, table, rotors, perm,
-    wave_ref, wave_rows_ref, spec_ref, lat_ref, lat_rows_ref, active_ref, weight_ref,
-    four, stack, small_sems, sems,
+    wave_hbm, spec_hbm, lat_rows_hbm, leg_hbm,
+    out_ref,
+    wave_ref, spec_ref, lat_rows_ref, leg, stack, small_sems, sems,
 ):
     pairs, coef, lat_total = leg.shape
-    lat_here = table.shape[0]
-    small = [
-        pltpu.make_async_copy(source, target, small_sems.at[n])
-        for n, (source, target) in enumerate(
-            (
-                (lat_rows_hbm, lat_rows_ref),
-                (wave_rows_hbm, wave_rows_ref),
-                (lat_hbm, lat_ref),
-                (active_hbm, active_ref),
-                (weight_hbm, weight_ref),
-                (wave_hbm, wave_ref),
-                (spec_hbm, spec_ref),
-            )
-        )
-    ]
-    copies = [pltpu.make_async_copy(leg_hbm.at[p], leg.at[p], sems.at[p]) for p in range(pairs)]
-    for copy in small + copies:
-        copy.start()
-    stack[...] = jnp.zeros_like(stack)
-    four[...] = jnp.zeros_like(four)
+    lat_here = lat_total // 256
+    small = start_copies(
+        ((lat_rows_hbm, lat_rows_ref), (spec_hbm, spec_ref), (wave_hbm, wave_ref)), small_sems
+    )
+    copies = start_copies([(leg_hbm.at[p], leg.at[p]) for p in range(pairs)], sems)
+    stack[120:128, :] = jnp.zeros((8, 256), F32)
     for copy in small:
         copy.wait()
-    fill_onehot(onehot, lat_rows_ref, lat_here)
-    fill_tables(table, rotors, wave_rows_ref, lat_ref, active_ref, weight_ref)
-    fill_perm(perm)
+    table = latitude_table(lat_rows_ref, lat_here)
     wide = lax.axis_index("wide")
     column = iota((2, coef), 1)
+    lefts = []
     for p in range(pairs):
-        first = wave_ref[wide * 2 * pairs + 2 * p]
-        own = column < coef - 1 - first
+        own = column < coef - 1 - wave_ref[wide * 2 * pairs + 2 * p]
         rows = spec_ref[p].astype(F32)
         nothing = jnp.zeros_like(rows)
-        left = jnp.concatenate(
-            [
-                jnp.where(own, rows, nothing),
-                jnp.where(own, nothing, rows),
-                nothing,
-                nothing,
-            ],
-            0,
-        ).astype(BF16)
-        copies[p].wait()
-        result = jnp.dot(left, leg[p], preferred_element_type=F32)
-        for s in range(2):
+        used = [jnp.where(own, rows, nothing), jnp.where(own, nothing, rows)]
+        idle = [nothing, nothing]
+        lefts.append(jnp.concatenate(idle + used if p % 2 else used + idle, 0).astype(BF16))
+    for group in range((pairs + 1) // 2):
+        total = jnp.zeros((8, lat_total), F32)
+        for p in group_pairs(group, pairs):
+            copies[p].wait()
+            total = total + jnp.dot(lefts[p], leg[p], preferred_element_type=F32)
+        total = total.astype(BF16).astype(F32)
+        tiles = [total[:, k * 128 : (k + 1) * 128] for k in range(lat_total // 128)]
+        for i in range(lat_here):
+            at = i * 24 + group * 8
+            for h in range(2):
+                index = jnp.broadcast_to(table[i : i + 1, h * 128 : (h + 1) * 128], (8, 128))
+                stack[at : at + 8, h * 128 : (h + 1) * 128] = gather_tiles(tiles, index)
+    out_ref[...] = stack[...].T
+
+
+def prepare_kernel(
+    wave_hbm, wave_rows_hbm, lat_hbm, lat_rows_hbm, active_hbm, weight_hbm, leg_hbm,
+    table, rotors, perm, position, owners, turned_hbm,
+    wave_ref, wave_rows_ref, lat_ref, lat_rows_ref, active_ref, weight_ref, leg, turned,
+    small_sems, load_sems, store_sems,
+):
+    lat_here = table.shape[0]
+    pairs, coef, lat_total = leg.shape
+    copies = start_copies(
+        (
+            (lat_rows_hbm, lat_rows_ref),
+            (wave_rows_hbm, wave_rows_ref),
+            (wave_hbm, wave_ref),
+            (lat_hbm, lat_ref),
+            (active_hbm, active_ref),
+            (weight_hbm, weight_ref),
+        ),
+        small_sems,
+    )
+    loads = start_copies([(leg_hbm.at[p], leg.at[p]) for p in range(pairs)], load_sems)
+    fill_perm(perm)
+    for copy in copies:
+        copy.wait()
+    fill_tables(table, rotors, wave_rows_ref, lat_ref, active_ref, weight_ref)
+    where_from = latitude_table(lat_rows_ref, lat_here)
+    lanes = iota((128, 128), 1).astype(F32)
+    position[...] = jnp.zeros_like(position)
+    for block in range(lat_here * 2):
+        latitude = iota((128, 128), 0) + block * 128
+        found = jnp.zeros((128, 128), F32)
+        for i in range(lat_here):
+            for h in range(2):
+                row = where_from[i : i + 1, h * 128 : (h + 1) * 128]
+                hit = jnp.broadcast_to(row, (128, 128)) == latitude
+                found = jnp.where(hit, lanes + (i * 256 + h * 128), found)
+        total = jnp.sum(found.T, axis=0, keepdims=True)
+        position[block : block + 1, :] = total.astype(I32)
+    wide = lax.axis_index("wide")
+    column = iota((1, owners.shape[1]), 1)
+    owners[...] = jnp.zeros_like(owners)
+    for p in range(pairs):
+        own = column < coef - 1 - wave_ref[wide * 2 * pairs + 2 * p]
+        owners[p : p + 1, :] = jnp.where(own, 1.0, 0.0)
+    stores = []
+    for p in range(pairs):
+        loads[p].wait()
+        for at in range(0, coef, 128):
+            if at + 128 <= coef:
+                block = leg[p, at : at + 128, :]
+            else:
+                block = jnp.broadcast_to(leg[p, at : at + 1, :], (128, lat_total))
+            turned[p, :, at : at + 128] = block.T
+        stores += start_copies(
+            [(turned.at[p], turned_hbm.at[p])], store_sems.at[pl.ds(p, 1)]
+        )
+    for copy in stores:
+        copy.wait()
+
+
+def direct_kernel(recv_ref, position, owners, turned, out_ref):
+    pairs, _, _, coef = out_ref.shape
+    lat_total = turned.shape[1]
+    lat_here = lat_total // 256
+    rows = recv_ref[...].T
+    for group in range((pairs + 1) // 2):
+        tiles = []
+        for i in range(lat_here):
+            at = i * 24 + group * 8
+            tiles += [rows[at : at + 8, :128], rows[at : at + 8, 128:]]
+        ordered = []
+        for block in range(lat_total // 128):
+            index = jnp.broadcast_to(position[block : block + 1, :], (8, 128))
+            ordered.append(gather_tiles(tiles, index))
+        left = jnp.concatenate(ordered, 1).astype(BF16)
+        for p in group_pairs(group, pairs):
+            own = owners[p : p + 1, :coef] > 0.0
+            result = jnp.dot(left, turned[p], preferred_element_type=F32)
+            at = 4 * (p % 2)
             for r in range(2):
-                row = s * 12 + r * pairs + p
-                four[row : row + 1, :] = result[2 * s + r : 2 * s + r + 1, :]
-    placed = jnp.dot(four[...].astype(BF16), onehot[...], preferred_element_type=F32)
-    for i in range(lat_here):
-        for s in range(2):
-            stack[s * 64 + i * 12 : s * 64 + i * 12 + 12, :] = placed[
-                s * 12 : s * 12 + 12, i * 256 : (i + 1) * 256
-            ]
-    out_ref[...] = stack[...].T
-
-
-def direct_kernel(wave_ref, recv_ref, onehot, leg, out_ref):
-    pairs, coef, lat_total = leg.shape
-    lat_here = lat_total // 256
-    wide = lax.axis_index("wide")
-    turned = recv_ref[...].T
-    pieces = []
-    for i in range(lat_here):
-        pieces.append(
-            jnp.concatenate(
-                [turned[i * 12 : i * 12 + 12, :], turned[64 + i * 12 : 64 + i * 12 + 12, :]], 0
-            )
-        )
-    slots = jnp.concatenate(pieces, 1).astype(BF16)
-    ordered = lax.dot_general(slots, onehot[...], NT, preferred_element_type=F32)
-    column = iota((1, coef), 1)
-    for p in range(pairs):
-        first = wave_ref[wide * 2 * pairs + 2 * p]
-        own = column < coef - 1 - first
-        left = jnp.concatenate(
-            [
-                ordered[s * 12 + r * pairs + p : s * 12 + r * pairs + p + 1, :]
-                for s in range(2)
-                for r in range(2)
-            ]
-            + [jnp.zeros((4, lat_total), F32)],
-            0,
-        ).astype(BF16)
-        result = lax.dot_general(left, leg[p], NT, preferred_element_type=F32)
-        for r in range(2):
-            out_ref[p, r, :, :] = jnp.where(own, result[r : r + 1, :], result[2 + r : 3 + r, :])
+                out_ref[p, r, :, :] = jnp.where(
+                    own,
+                    result[at + r : at + r + 1, :coef],
+                    result[at + 2 + r : at + 3 + r, :coef],
+                )
 
 
 def fourier_kernel(
-    recv_ref, table, rotors, perm, wind_ref, grid_ref, out_ref, four, left, backs,
+    recv_ref, table, rotors, perm, wind_ref, grid_hbm, out_ref,
+    flat, four, left, backs, grid_ref, sems,
 ):
     lat_here, levels, points = wind_ref.shape
     half = table.shape[2] // 2
     blocks = half // 128
     outer = points // 128
-    turned = recv_ref[...].T.astype(BF16)
-    joined = jnp.concatenate([turned[:64, :], turned[64:, :]], 1)
+    for h in range(2):
+        flat[h * 128 : (h + 1) * 128, :] = recv_ref[h * 128 : (h + 1) * 128, :].T
+    joined = jnp.concatenate(
+        [
+            jnp.concatenate(
+                [
+                    flat[pl.ds(h * 128 + 2 * s + r, 32, stride=4), :]
+                    for s in range(2)
+                    for h in range(2)
+                ],
+                1,
+            )
+            for r in range(2)
+        ],
+        0,
+    ).astype(BF16)
     spread = jnp.dot(joined, perm[...], preferred_element_type=F32)
     for l in range(4):
         for copy in range(2):
@@ -244,15 +300,16 @@
         at = (i * blocks + p) * 8 + n
         return jnp.broadcast_to(rotors[at : at + 1, :], (8, 128))
 
+    copies = []
     for i in range(lat_here):
         for p in range(blocks):
             cosx = jnp.where(upper, 1.0, rotor(i, p, 0))
             sinx = jnp.where(upper, 0.0, rotor(i, p, 1))
             cos2, sin2, scale = (rotor(i, p, n) for n in (2, 3, 4))
             lo, hi = p * 128, half + p * 128
-            at = (i * 12 + p) * 8
+            at = (i * 6 + p) * 8
             real = four[at : at + 8, :] * scale
-            at = (i * 12 + blocks + p) * 8
+            at = (32 + i * 6 + p) * 8
             imag = four[at : at + 8, :] * scale
             real, imag = real * cosx - imag * sinx, real * sinx + imag * cosx
             held = []
@@ -275,6 +332,7 @@
         for a in range(outer):
             grid_ref[i, :, a * 128 : (a + 1) * 128] = values[a * 4 : a * 4 + 4, :].astype(BF16)
             winds.append(wind_ref[i, :, a * 128 : (a + 1) * 128].astype(F32))
+        copies += start_copies([(grid_ref.at[i], grid_hbm.at[i])], sems.at[pl.ds(i, 1)])
         product = (values * jnp.concatenate(winds, 0)).astype(BF16)
         sums = jnp.dot(product, table[i], preferred_element_type=F32)
         for p in range(blocks):
@@ -294,14 +352,24 @@
             real = real + pltpu.roll(real, 4, 0)
             imag = imag + pltpu.roll(imag, 4, 0)
             both = jnp.where(upper, real, -imag) * gain
-            at = (i * 12 + p) * 4
+            at = (i * 6 + p) * 4
             backs[at : at + 4, :] = both[0:4, :]
-            at = (i * 12 + blocks + p) * 4
+            at = (32 + i * 6 + p) * 4
             backs[at : at + 4, :] = both[4:8, :]
 
     joined = jnp.concatenate([backs[pl.ds(l, 64, stride=4), :] for l in range(4)], 1)
     spread = lax.dot_general(joined.astype(BF16), perm[...], NT, preferred_element_type=F32)
-    out_ref[...] = jnp.concatenate([spread[:, :256], spread[:, 256:]], 0).T
+    for r in range(2):
+        for s in range(2):
+            for h in range(2):
+                lo = s * 256 + h * 128
+                flat[pl.ds(h * 128 + 2 * s + r, 32, stride=4), :] = spread[
+                    r * 32 : r * 32 + 32, lo : lo + 128
+                ]
+    for h in range(2):
+        out_ref[h * 128 : (h + 1) * 128, :] = flat[h * 128 : (h + 1) * 128, :].T
+    for copy in copies:
+        copy.wait()
 
 
 def vmem():
@@ -310,10 +378,6 @@
 
 def hbm():
     return pl.BlockSpec(memory_space=pltpu.HBM)
-
-
-def smem():
-    return pl.BlockSpec(memory_space=pltpu.SMEM)
 
 
 def in_hbm(x):
@@ -337,37 +401,56 @@
     wave_rows = wave_order.reshape(wave_order.shape[0] // 128, 128)
 
     waves = wave_order.shape[0]
-    operands = (
-        wave_order, wave_rows, spec_in.reshape(pairs, 2, coef), lat_order, lat_rows, active,
-        lat_weight, legendre,
-    )
-    outgoing, leg_here, onehot, table, rotors, perm = pl.pallas_call(
+    wide_coef = (coef + 127) // 128 * 128
+    operands = (wave_order, spec_in.reshape(pairs, 2, coef), lat_rows, legendre)
+    outgoing = pl.pallas_call(
         inverse_kernel,
         name="legendre_inverse",
+        out_shape=jax.ShapeDtypeStruct((devices, 128), F32),
+        in_specs=[hbm()] * len(operands),
+        out_specs=vmem(),
+        scratch_shapes=[
+            pltpu.SMEM(wave_order.shape, I32),
+            pltpu.VMEM((pairs, 2, coef), BF16),
+            pltpu.VMEM(lat_rows.shape, I32),
+            pltpu.VMEM(legendre.shape, BF16),
+            pltpu.VMEM((128, devices), F32),
+            pltpu.SemaphoreType.DMA((3,)),
+            pltpu.SemaphoreType.DMA((pairs,)),
+        ],
+        compiler_params=limit,
+    )(*(in_hbm(x) for x in operands))
+
+    arrived = exchange(outgoing)
+    operands = (wave_order, wave_rows, lat_order, lat_rows, active, lat_weight, legendre)
+    table, rotors, perm, position, owners, turned = pl.pallas_call(
+        prepare_kernel,
+        name="prepare",
         out_shape=(
-            jax.ShapeDtypeStruct((devices, 128), F32),
-            jax.ShapeDtypeStruct(legendre.shape, BF16),
-            jax.ShapeDtypeStruct((lat_total, lat_total), BF16),
             jax.ShapeDtypeStruct((lat_here, 128, 2 * waves), BF16),
             jax.ShapeDtypeStruct((lat_here * waves // 128 * 8, 128), F32),
             jax.ShapeDtypeStruct((512, 512), BF16),
+            jax.ShapeDtypeStruct((16, 128), I32),
+            jax.ShapeDtypeStruct((8, wide_coef), F32),
+            pltpu.HBM((pairs, lat_total, wide_coef), BF16),
         ),
         in_specs=[hbm()] * len(operands),
-        out_specs=(vmem(),) * 6,
+        out_specs=(vmem(),) * 5 + (hbm(),),
         scratch_shapes=[
             pltpu.SMEM(wave_order.shape, I32),
             pltpu.VMEM(wave_rows.shape, I32),
-            pltpu.VMEM((pairs, 2, coef), BF16),
             pltpu.SMEM(lat_order.shape, I32),
             pltpu.VMEM(lat_rows.shape, I32),
             pltpu.SMEM(active.shape, I32),
             pltpu.SMEM(lat_weight.shape, F32),
-            pltpu.VMEM((24, lat_total), F32),
-            pltpu.VMEM((128, devices), F32),
-            pltpu.SemaphoreType.DMA((7,)),
+            pltpu.VMEM(legendre.shape, BF16),
+            pltpu.VMEM((pairs, lat_total, wide_coef), BF16),
+            pltpu.SemaphoreType.DMA((6,)),
+            pltpu.SemaphoreType.DMA((pairs,)),
             pltpu.SemaphoreType.DMA((pairs,)),
         ],
         compiler_params=limit,
+        cost_estimate=BUSY,
     )(*(in_hbm(x) for x in operands))
 
     grid, outgoing = pl.pallas_call(
@@ -378,23 +461,28 @@
             jax.ShapeDtypeStruct((devices, 128), F32),
         ),
         in_specs=[vmem()] * 5,
-        out_specs=(vmem(), vmem()),
+        out_specs=(hbm(), vmem()),
         scratch_shapes=[
+            pltpu.VMEM((devices, 128), F32),
             pltpu.VMEM((512, 128), F32),
             pltpu.VMEM((lat_here, points // 32, 2 * waves), BF16),
             pltpu.VMEM((256, 128), F32),
+            pltpu.VMEM(wind.shape, BF16),
+            pltpu.SemaphoreType.DMA((lat_here,)),
         ],
         compiler_params=limit,
-    )(exchange(outgoing), table, rotors, perm, wind)
-
+        cost_estimate=BUSY,
+    )(arrived, table, rotors, perm, wind)
+
+    arrived = exchange(outgoing)
     spec_out = pl.pallas_call(
         direct_kernel,
         name="legendre_direct",
         out_shape=jax.ShapeDtypeStruct((pairs, 2, 1, coef), F32),
-        in_specs=[smem(), vmem(), vmem(), vmem()],
+        in_specs=[vmem()] * 4,
         out_specs=vmem(),
         compiler_params=limit,
-    )(wave_order, exchange(outgoing), onehot, leg_here)
+    )(arrived, position, owners, turned)
     return (grid, spec_out)
 
 

time: 61.8 us -> 59.9 us (0.969)
  blocking collectives: 46.5 us -> 20.5 us
  starting transfers between devices: 0 us -> 15.7 us
  waiting for transfers between devices: 0 us -> 5.82 us
  Pallas kernels: 14.5 us -> 17 us
    all_to_all x2 -> x1, blocking collectives: 46.5 us -> 20.5 us  [exchange(): lax.all_to_all(rows.reshape(count, 1, width), ('wide', 'lev'), split_axis...]
    all_to_all x0 -> x1, starting transfers between devices: none -> 15.7 us  [exchange(): lax.all_to_all(rows.reshape(count, 1, width), ('wide', 'lev'), split_axis...]
    all_to_all x0 -> x1, waiting for transfers between devices: none -> 5.82 us  [exchange(): lax.all_to_all(rows.reshape(count, 1, width), ('wide', 'lev'), split_axis...]
    pallas_call x1 -> x2, Pallas kernels: 7.25 us -> 12.2 us  [the longest x1 6.91 us: shards(): pl.pallas_call(prepare_kernel, name='prepare', out_shape=(jax.ShapeDtypeS...]
    pallas_call x1, Pallas kernels: 4.46 us -> 2.23 us  [shards(): pl.pallas_call(direct_kernel, name='legendre_direct', out_shape=jax.Shape...]
  transfers between devices with their start and end apart: 0 -> 1, of which waited for: 0 -> 1; matrix products, arithmetic and copies ran while one was open for 0% -> 0% of each run, Pallas kernels for 0% -> 12%
where the time goes in v3:
time: 59.9 us; the launch traced here: 59.7 us
  blocking collectives  20.5 us (34%)
  Pallas kernels  17 us (28%)
  starting transfers between devices  15.7 us (26%)
  waiting for transfers between devices  5.82 us (10%)
  between operations  0.67 us (1%)
    all_to_all x1, blocking collectives, exchange(): lax.all_to_all(rows.reshape(count, 1, width), ('wide', 'lev'), split_axis...  20.5 us
    all_to_all x1, starting transfers between devices, exchange(): lax.all_to_all(rows.reshape(count, 1, width), ('wide', 'lev'), split_axis...  15.7 us
    pallas_call x1, Pallas kernels, shards(): pl.pallas_call(prepare_kernel, name='prepare', out_shape=(jax.ShapeDtypeS...  6.91 us
    all_to_all x1, waiting for transfers between devices, exchange(): lax.all_to_all(rows.reshape(count, 1, width), ('wide', 'lev'), split_axis...  5.82 us
    pallas_call x1, Pallas kernels, shards(): pl.pallas_call(inverse_kernel, name='legendre_inverse', out_shape=jax.Sha...  5.25 us
    pallas_call x1, Pallas kernels, shards(): pl.pallas_call(fourier_kernel, name='fourier', out_shape=(jax.ShapeDtypeS...  2.63 us
    pallas_call x1, Pallas kernels, shards(): pl.pallas_call(direct_kernel, name='legendre_direct', out_shape=jax.Shape...  2.23 us
  transfers between devices with their start and end apart: 1, of which 1 were waited for; matrix products, arithmetic and copies ran while one was open for 0% of the time, Pallas kernels for 12%

profile of v3, /device:TPU:1, one launch (start us, length us, event | category | flops | bytes accessed | tf_op | source)
XLA Modules:
  0.0 59.7 jit_solution(7019526073148552551)
XLA Ops:
  0.6 5.3 %legendre_inverse.1 = f32[256,128]{1,0:T(8,128)} custom-call(s32[640]{0:T(1024)} %wave_hbm.3, bf16[5,2,641]{2,1,0:T(2,128)(2,1)} %bitcast.14, s32[10,128]{1,0:T(8,128)} %bitcast.15, bf16[5,641,1280]{2,1,0:T(8,128)(2,1)} %leg_hbm.3), custom_call_target="tpu_custom_call" | custom-call | tf_op jit(solution)/shard_map/legendre_inverse/pallas_call | solution.py:406
  5.9 0.0 copy-start.1
  5.9 15.7 %all-to-all-start = ((f32[256,1,128]{2,1,0:T(1,128)}), f32[256,1,128]{2,1,0:T(1,128)S(1)}, u32[]{:S(2)}, u32[]{:S(2)}) async-start(f32[256,1,128]{2,1,0:T(1,128)} %bitcast.3), calls=%async_computation | async-start | bytes 262144 | tf_op jit(solution)/shard_map/all_to_all | solution.py:389
  21.6 6.9 %prepare.1 = (bf16[5,128,1280]{2,1,0:T(8,128)(2,1)S(1)}, f32[200,128]{1,0:T(8,128)S(1)}, bf16[512,512]{1,0:T(8,128)(2,1)S(1)}, s32[16,128]{1,0:T(8,128)S(1)}, f3...) custom-call(s32[640]{0:T(1024)} %wave_hbm.3, s32[5,128]{1,0:T(8,128)} %bitcast.17, s32[1280]{0:T(1024)} %lat_hbm.1, ...), custom_call_target="tpu_custom_call" | custom-call | flops 4000000000 | bytes 16000000 | tf_op jit(solution)/shard_map/prepare/pallas_call | solution.py:426
  28.5 5.8 %all-to-all-done = f32[256,1,128]{2,1,0:T(1,128)S(1)} async-done(((f32[256,1,128]{2,1,0:T(1,128)}), f32[256,1,128]{2,1,0:T(1,128)S(1)}, u32[]{:S(2)}, u32[]{:S(2)}) %all-to-all-start) | async-done | bytes 131104 | tf_op jit(solution)/shard_map/all_to_all | solution.py:389
  34.3 0.0 copy-start
  34.3 0.0 copy-done.1
  34.3 2.6 %fourier.1 = (bf16[5,4,2560]{2,1,0:T(4,128)(2,1)}, f32[256,128]{1,0:T(8,128)S(1)}) custom-call(f32[256,128]{1,0:T(8,128)S(1)} %bitcast.12, bf16[5,128,1280]{2,1,0:T(8,128)(2,1)S(1)} %get-tuple-element.10.table, f32[200,128]{1,0:T(8,128)S(1)} %get-tuple-element.11.rotors, bf16[512,512]{1,0:T(8,128)(2,1)S(1)} %get-tuple-element.12.perm, ...), custom_call_target="tpu_custom_call" | custom-call | flops 4000000000 | bytes 16000000 | tf_op jit(solution)/shard_map/fourier/pallas_call | solution.py:456
  37.0 20.5 %all_to_all.10 = f32[256,1,128]{2,1,0:T(1,128)S(1)} all-to-all(f32[256,1,128]{2,1,0:T(1,128)S(1)} %bitcast.13), channel_id=1, replica_groups=mesh['wide'=64,'lev'=4] {'wide','lev'}, dimensions={0} | all-to-all | bytes 262144 | tf_op jit(solution)/shard_map/all_to_all | solution.py:389
  57.5 0.0 copy-done
  57.5 2.2 %legendre_direct.1 = f32[5,2,1,641]{3,2,1,0:T(1,128)} custom-call(f32[256,128]{1,0:T(8,128)S(1)} %bitcast.11, s32[16,128]{1,0:T(8,128)S(1)} %get-tuple-element.15.position, f32[8,768]{1,0:T(8,128)S(1)} %get-tuple-element.16.owners, bf16[5,1280,768]{2,1,0:T(8,128)(2,1)S(1)} %copy-done), custom_call_target="tpu_custom_call" | custom-call | tf_op jit(solution)/shard_map/legendre_direct/pallas_call | solution.py:478
Async XLA Ops:
  5.9 28.4 %copy-start.1 = (bf16[5,4,2560]{2,1,0:T(4,128)(2,1)S(1)}, bf16[5,4,2560]{2,1,0:T(4,128)(2,1)}, u32[]{:S(2)}) copy-start(bf16[5,4,2560]{2,1,0:T(4,128)(2,1)} %wind_ref.1) | copy-start | bytes 307204
  5.9 28.4 %all-to-all-start = ((f32[256,1,128]{2,1,0:T(1,128)}), f32[256,1,128]{2,1,0:T(1,128)S(1)}, u32[]{:S(2)}, u32[]{:S(2)}) async-start(f32[256,1,128]{2,1,0:T(1,128)} %bitcast.3), calls=%async_computation | async-start | bytes 262144 | tf_op jit(solution)/shard_map/all_to_all | solution.py:389
  34.3 23.2 %copy-start = (bf16[5,1280,768]{2,1,0:T(8,128)(2,1)S(1)}, bf16[5,1280,768]{2,1,0:T(8,128)(2,1)}, u32[]{:S(2)}) copy-start(bf16[5,1280,768]{2,1,0:T(8,128)(2,1)} %get-tuple-element.17.turned) | copy-start | bytes 29491204

commit v4 on v3

--- a/solution.py
+++ b/solution.py
@@ -11,7 +11,7 @@
 BF16 = jnp.bfloat16
 I32 = jnp.int32
 NT = (((1,), (1,)), ((), ()))
-BUSY = pl.CostEstimate(flops=4_000_000_000, bytes_accessed=16_000_000, transcendentals=0)
+FLIGHT = 5
 
 
 def iota(shape, axis):
@@ -86,154 +86,147 @@
     return pick(wave_rows_ref, 0, blocks, index)
 
 
-def fill_tables(table, rotors, wave_rows_ref, lato_ref, active_ref, weight_ref):
+def fill_tables(table, rotors, waves, i, lato_ref, active_ref, weight_ref):
     lat_here = table.shape[0]
-    blocks = wave_rows_ref.shape[0]
-    half = blocks * 128
+    half = table.shape[2] // 2
+    blocks = half // 128
     row = iota((8, 128), 0)
-    waves = wave_table(wave_rows_ref, blocks)
     waves_f = waves.astype(F32)
     steps_low = row.astype(F32)
     steps_high = jnp.where(row == 0, 8.0, jnp.where(row == 1, 128.0, 256.0))
     first_slot = (lax.axis_index("wide") * lax.axis_size("lev") + lax.axis_index("lev")) * lat_here
-    for i in range(lat_here):
-        lat = lato_ref[first_slot + i]
-        live = jnp.full((8, 128), active_ref[lat], I32)
-        cells = (live * 4).astype(F32)
-        inverse = 1.0 / cells
-        gain = jnp.full((8, 128), weight_ref[lat], F32) / cells
-        for p in range(blocks):
-            wave = jnp.broadcast_to(waves_f[p : p + 1, :], (8, 128))
-            alive = jnp.broadcast_to(waves[p : p + 1, :], (8, 128)) < live
-            angles = []
-            for steps in (steps_low, steps_high):
-                phase = wave * steps
-                rest = phase - jnp.round(phase * inverse) * cells
-                angles.append(turn(rest * inverse))
-            (cos_b, sin_b), (cos_h, sin_h) = angles
-            cos8 = jnp.broadcast_to(cos_h[0:1, :], (8, 128))
-            sin8 = jnp.broadcast_to(sin_h[0:1, :], (8, 128))
-            lo, hi = p * 128, half + p * 128
-            held = []
-            for b in range(16):
-                held.append((cos_b, sin_b))
-                if b % 2:
-                    at = (b - 1) * 8
-                    table[i, at : at + 16, lo : lo + 128] = jnp.concatenate(
-                        [held[b - 1][0], cos_b], 0
-                    ).astype(BF16)
-                    table[i, at : at + 16, hi : hi + 128] = jnp.concatenate(
-                        [held[b - 1][1], sin_b], 0
-                    ).astype(BF16)
-                if b < 15:
-                    cos_b, sin_b = cos_b * cos8 - sin_b * sin8, sin_b * cos8 + cos_b * sin8
-            scale = jnp.where(alive, jnp.where(wave == 0.0, 1.0, 2.0), 0.0)
-            lines = (
-                cos_h[1:2, :], sin_h[1:2, :], cos_h[2:3, :], sin_h[2:3, :],
-                scale[0:1, :], jnp.where(alive, gain, 0.0)[0:1, :], cells[0:1, :],
-            )
-            at = (i * blocks + p) * 8
-            for n, line in enumerate(lines):
-                rotors[at + n : at + n + 1, :] = line
+    lat = lato_ref[first_slot + i]
+    live = jnp.full((8, 128), active_ref[lat], I32)
+    cells = (live * 4).astype(F32)
+    inverse = 1.0 / cells
+    gain = jnp.full((8, 128), weight_ref[lat], F32) / cells
+    for p in range(blocks):
+        wave = jnp.broadcast_to(waves_f[p : p + 1, :], (8, 128))
+        alive = jnp.broadcast_to(waves[p : p + 1, :], (8, 128)) < live
+        angles = []
+        for steps in (steps_low, steps_high):
+            phase = wave * steps
+            rest = phase - jnp.round(phase * inverse) * cells
+            angles.append(turn(rest * inverse))
+        (cos_b, sin_b), (cos_h, sin_h) = angles
+        cos8 = jnp.broadcast_to(cos_h[0:1, :], (8, 128))
+        sin8 = jnp.broadcast_to(sin_h[0:1, :], (8, 128))
+        lo, hi = p * 128, half + p * 128
+        held = []
+        for b in range(16):
+            held.append((cos_b, sin_b))
+            if b % 2:
+                at = (b - 1) * 8
+                table[i, at : at + 16, lo : lo + 128] = jnp.concatenate(
+                    [held[b - 1][0], cos_b], 0
+                ).astype(BF16)
+                table[i, at : at + 16, hi : hi + 128] = jnp.concatenate(
+                    [held[b - 1][1], sin_b], 0
+                ).astype(BF16)
+            if b < 15:
+                cos_b, sin_b = cos_b * cos8 - sin_b * sin8, sin_b * cos8 + cos_b * sin8
+        scale = jnp.where(alive, jnp.where(wave == 0.0, 1.0, 2.0), 0.0)
+        lines = (
+            cos_h[1:2, :], sin_h[1:2, :], cos_h[2:3, :], sin_h[2:3, :],
+            scale[0:1, :], jnp.where(alive, gain, 0.0)[0:1, :], cells[0:1, :],
+        )
+        at = (i * blocks + p) * 8
+        for n, line in enumerate(lines):
+            rotors[at + n : at + n + 1, :] = line
+
+
+def fill_position(position, where_from, lat_here):
+    rows = jnp.concatenate(
+        [where_from[i : i + 1, h * 128 : (h + 1) * 128] for i in range(lat_here) for h in range(2)],
+        1,
+    )
+    count = rows.shape[1]
+    number = iota((16, count), 1)
+    high = jnp.broadcast_to(rows >> 7, (16, count)) == iota((16, count), 0)
+    parts = [
+        jnp.where(high, part.astype(F32), 0.0).astype(BF16) for part in (number >> 4, number & 15)
+    ]
+    low = jnp.broadcast_to(rows & 127, (128, count)) == iota((128, count), 0)
+    found = lax.dot_general(
+        jnp.concatenate(parts, 0),
+        jnp.where(low, 1.0, 0.0).astype(BF16),
+        NT,
+        preferred_element_type=F32,
+    )
+    position[...] = (found[:16, :] * 16.0 + found[16:, :]).astype(I32)
+
+
+def turn_pair(turned, leg, p):
+    _, coef, lat_total = leg.shape
+    for at in range(0, coef, 128):
+        if at + 128 <= coef:
+            block = leg[p, at : at + 128, :]
+        else:
+            block = jnp.broadcast_to(leg[p, at : at + 1, :], (128, lat_total))
+        turned[p, :, at : at + 128] = block.T
 
 
 def inverse_kernel(
-    wave_hbm, spec_hbm, lat_rows_hbm, leg_hbm,
-    out_ref,
-    wave_ref, spec_ref, lat_rows_ref, leg, stack, small_sems, sems,
+    wave_hbm, wave_rows_hbm, spec_hbm, lat_hbm, lat_rows_hbm, active_hbm, weight_hbm, leg_hbm,
+    out_ref, leg, table, rotors, perm, position, owners,
+    wave_ref, wave_rows_ref, spec_ref, lat_ref, lat_rows_ref, active_ref, weight_ref,
+    stack, small_sems, sems,
 ):
-    pairs, coef, lat_total = leg.shape
+    pairs, coef, lat_total = leg_hbm.shape
     lat_here = lat_total // 256
     small = start_copies(
-        ((lat_rows_hbm, lat_rows_ref), (spec_hbm, spec_ref), (wave_hbm, wave_ref)), small_sems
-    )
-    copies = start_copies([(leg_hbm.at[p], leg.at[p]) for p in range(pairs)], sems)
+        (
+            (lat_rows_hbm, lat_rows_ref),
+            (wave_rows_hbm, wave_rows_ref),
+            (wave_hbm, wave_ref),
+            (spec_hbm, spec_ref),
+            (lat_hbm, lat_ref),
+            (active_hbm, active_ref),
+            (weight_hbm, weight_ref),
+        ),
+        small_sems,
+    )
+    copies = [pltpu.make_async_copy(leg_hbm.at[p], leg.at[p], sems.at[p]) for p in range(pairs)]
+    for copy in copies[:FLIGHT]:
+        copy.start()
     stack[120:128, :] = jnp.zeros((8, 256), F32)
+    fill_perm(perm)
+    owners[...] = jnp.zeros_like(owners)
     for copy in small:
         copy.wait()
-    table = latitude_table(lat_rows_ref, lat_here)
+    where_from = latitude_table(lat_rows_ref, lat_here)
+    fill_position(position, where_from, lat_here)
+    waves = wave_table(wave_rows_ref, wave_rows_ref.shape[0])
     wide = lax.axis_index("wide")
     column = iota((2, coef), 1)
     lefts = []
     for p in range(pairs):
         own = column < coef - 1 - wave_ref[wide * 2 * pairs + 2 * p]
+        owners[p : p + 1, :coef] = jnp.where(own[:1], 1.0, 0.0)
         rows = spec_ref[p].astype(F32)
         nothing = jnp.zeros_like(rows)
         used = [jnp.where(own, rows, nothing), jnp.where(own, nothing, rows)]
         idle = [nothing, nothing]
         lefts.append(jnp.concatenate(idle + used if p % 2 else used + idle, 0).astype(BF16))
-    for group in range((pairs + 1) // 2):
-        total = jnp.zeros((8, lat_total), F32)
-        for p in group_pairs(group, pairs):
-            copies[p].wait()
-            total = total + jnp.dot(lefts[p], leg[p], preferred_element_type=F32)
+    total = None
+    for p in range(pairs):
+        for i in range(p, lat_here, pairs):
+            fill_tables(table, rotors, waves, i, lat_ref, active_ref, weight_ref)
+        copies[p].wait()
+        if p + FLIGHT < pairs:
+            copies[p + FLIGHT].start()
+        result = jnp.dot(lefts[p], leg[p], preferred_element_type=F32)
+        total = total + result if p % 2 else result
+        if p % 2 == 0 and p < pairs - 1:
+            continue
         total = total.astype(BF16).astype(F32)
         tiles = [total[:, k * 128 : (k + 1) * 128] for k in range(lat_total // 128)]
         for i in range(lat_here):
-            at = i * 24 + group * 8
+            at = i * 24 + p // 2 * 8
             for h in range(2):
-                index = jnp.broadcast_to(table[i : i + 1, h * 128 : (h + 1) * 128], (8, 128))
+                index = jnp.broadcast_to(where_from[i : i + 1, h * 128 : (h + 1) * 128], (8, 128))
                 stack[at : at + 8, h * 128 : (h + 1) * 128] = gather_tiles(tiles, index)
     out_ref[...] = stack[...].T
-
-
-def prepare_kernel(
-    wave_hbm, wave_rows_hbm, lat_hbm, lat_rows_hbm, active_hbm, weight_hbm, leg_hbm,
-    table, rotors, perm, position, owners, turned_hbm,
-    wave_ref, wave_rows_ref, lat_ref, lat_rows_ref, active_ref, weight_ref, leg, turned,
-    small_sems, load_sems, store_sems,
-):
-    lat_here = table.shape[0]
-    pairs, coef, lat_total = leg.shape
-    copies = start_copies(
-        (
-            (lat_rows_hbm, lat_rows_ref),
-            (wave_rows_hbm, wave_rows_ref),
-            (wave_hbm, wave_ref),
-            (lat_hbm, lat_ref),
-            (active_hbm, active_ref),
-            (weight_hbm, weight_ref),
-        ),
-        small_sems,
-    )
-    loads = start_copies([(leg_hbm.at[p], leg.at[p]) for p in range(pairs)], load_sems)
-    fill_perm(perm)
-    for copy in copies:
-        copy.wait()
-    fill_tables(table, rotors, wave_rows_ref, lat_ref, active_ref, weight_ref)
-    where_from = latitude_table(lat_rows_ref, lat_here)
-    lanes = iota((128, 128), 1).astype(F32)
-    position[...] = jnp.zeros_like(position)
-    for block in range(lat_here * 2):
-        latitude = iota((128, 128), 0) + block * 128
-        found = jnp.zeros((128, 128), F32)
-        for i in range(lat_here):
-            for h in range(2):
-                row = where_from[i : i + 1, h * 128 : (h + 1) * 128]
-                hit = jnp.broadcast_to(row, (128, 128)) == latitude
-                found = jnp.where(hit, lanes + (i * 256 + h * 128), found)
-        total = jnp.sum(found.T, axis=0, keepdims=True)
-        position[block : block + 1, :] = total.astype(I32)
-    wide = lax.axis_index("wide")
-    column = iota((1, owners.shape[1]), 1)
-    owners[...] = jnp.zeros_like(owners)
-    for p in range(pairs):
-        own = column < coef - 1 - wave_ref[wide * 2 * pairs + 2 * p]
-        owners[p : p + 1, :] = jnp.where(own, 1.0, 0.0)
-    stores = []
-    for p in range(pairs):
-        loads[p].wait()
-        for at in range(0, coef, 128):
-            if at + 128 <= coef:
-                block = leg[p, at : at + 128, :]
-            else:
-                block = jnp.broadcast_to(leg[p, at : at + 1, :], (128, lat_total))
-            turned[p, :, at : at + 128] = block.T
-        stores += start_copies(
-            [(turned.at[p], turned_hbm.at[p])], store_sems.at[pl.ds(p, 1)]
-        )
-    for copy in stores:
-        copy.wait()
 
 
 def direct_kernel(recv_ref, position, owners, turned, out_ref):
@@ -264,7 +257,7 @@
 
 
 def fourier_kernel(
-    recv_ref, table, rotors, perm, wind_ref, grid_hbm, out_ref,
+    recv_ref, table, rotors, perm, wind_ref, leg, grid_hbm, out_ref, turned,
     flat, four, left, backs, grid_ref, sems,
 ):
     lat_here, levels, points = wind_ref.shape
@@ -325,6 +318,8 @@
                     ).astype(BF16)
                 if a < outer // 2 - 1:
                     real, imag = real * cos2 - imag * sin2, real * sin2 + imag * cos2
+        for p in range(i, leg.shape[0], lat_here):
+            turn_pair(turned, leg, p)
         values = lax.dot_general(left[i], table[i], NT, preferred_element_type=F32)
         cells = jnp.broadcast_to(rotors[i * blocks * 8 + 6 : i * blocks * 8 + 7, :], point.shape)
         values = jnp.where(point < cells, values, 0.0).astype(BF16).astype(F32)
@@ -402,66 +397,50 @@
 
     waves = wave_order.shape[0]
     wide_coef = (coef + 127) // 128 * 128
-    operands = (wave_order, spec_in.reshape(pairs, 2, coef), lat_rows, legendre)
-    outgoing = pl.pallas_call(
+    operands = (
+        wave_order, wave_rows, spec_in.reshape(pairs, 2, coef), lat_order, lat_rows, active,
+        lat_weight, legendre,
+    )
+    outgoing, leg_here, table, rotors, perm, position, owners = pl.pallas_call(
         inverse_kernel,
         name="legendre_inverse",
-        out_shape=jax.ShapeDtypeStruct((devices, 128), F32),
-        in_specs=[hbm()] * len(operands),
-        out_specs=vmem(),
-        scratch_shapes=[
-            pltpu.SMEM(wave_order.shape, I32),
-            pltpu.VMEM((pairs, 2, coef), BF16),
-            pltpu.VMEM(lat_rows.shape, I32),
-            pltpu.VMEM(legendre.shape, BF16),
-            pltpu.VMEM((128, devices), F32),
-            pltpu.SemaphoreType.DMA((3,)),
-            pltpu.SemaphoreType.DMA((pairs,)),
-        ],
-        compiler_params=limit,
-    )(*(in_hbm(x) for x in operands))
-
-    arrived = exchange(outgoing)
-    operands = (wave_order, wave_rows, lat_order, lat_rows, active, lat_weight, legendre)
-    table, rotors, perm, position, owners, turned = pl.pallas_call(
-        prepare_kernel,
-        name="prepare",
         out_shape=(
+            jax.ShapeDtypeStruct((devices, 128), F32),
+            jax.ShapeDtypeStruct(legendre.shape, BF16),
             jax.ShapeDtypeStruct((lat_here, 128, 2 * waves), BF16),
             jax.ShapeDtypeStruct((lat_here * waves // 128 * 8, 128), F32),
             jax.ShapeDtypeStruct((512, 512), BF16),
             jax.ShapeDtypeStruct((16, 128), I32),
             jax.ShapeDtypeStruct((8, wide_coef), F32),
-            pltpu.HBM((pairs, lat_total, wide_coef), BF16),
         ),
         in_specs=[hbm()] * len(operands),
-        out_specs=(vmem(),) * 5 + (hbm(),),
+        out_specs=(vmem(),) * 7,
         scratch_shapes=[
             pltpu.SMEM(wave_order.shape, I32),
             pltpu.VMEM(wave_rows.shape, I32),
+            pltpu.VMEM((pairs, 2, coef), BF16),
             pltpu.SMEM(lat_order.shape, I32),
             pltpu.VMEM(lat_rows.shape, I32),
             pltpu.SMEM(active.shape, I32),
             pltpu.SMEM(lat_weight.shape, F32),
-            pltpu.VMEM(legendre.shape, BF16),
-            pltpu.VMEM((pairs, lat_total, wide_coef), BF16),
-            pltpu.SemaphoreType.DMA((6,)),
-            pltpu.SemaphoreType.DMA((pairs,)),
+            pltpu.VMEM((128, devices), F32),
+            pltpu.SemaphoreType.DMA((7,)),
             pltpu.SemaphoreType.DMA((pairs,)),
         ],
         compiler_params=limit,
-        cost_estimate=BUSY,
     )(*(in_hbm(x) for x in operands))
-
-    grid, outgoing = pl.pallas_call(
+    arrived = exchange(outgoing)
+
+    grid, outgoing, turned = pl.pallas_call(
         fourier_kernel,
         name="fourier",
         out_shape=(
             jax.ShapeDtypeStruct(wind.shape, BF16),
             jax.ShapeDtypeStruct((devices, 128), F32),
+            jax.ShapeDtypeStruct((pairs, lat_total, wide_coef), BF16),
         ),
-        in_specs=[vmem()] * 5,
-        out_specs=(hbm(), vmem()),
+        in_specs=[vmem()] * 6,
+        out_specs=(hbm(), vmem(), vmem()),
         scratch_shapes=[
             pltpu.VMEM((devices, 128), F32),
             pltpu.VMEM((512, 128), F32),
@@ -471,8 +450,7 @@
             pltpu.SemaphoreType.DMA((lat_here,)),
         ],
         compiler_params=limit,
-        cost_estimate=BUSY,
-    )(arrived, table, rotors, perm, wind)
+    )(arrived, table, rotors, perm, wind, leg_here)
 
     arrived = exchange(outgoing)
     spec_out = pl.pallas_call(

time: 59.9 us -> 57 us (0.952)
  blocking collectives: 20.5 us -> 46.5 us
  starting transfers between devices: 15.7 us -> 0 us
  Pallas kernels: 17 us -> 9.69 us
  waiting for transfers between devices: 5.82 us -> 0 us
    all_to_all x1 -> x2, blocking collectives: 20.5 us -> 46.5 us  [exchange(): lax.all_to_all(rows.reshape(count, 1, width), ('wide', 'lev'), split_axis...]
    all_to_all x1 -> x0, starting transfers between devices: 15.7 us -> none  [exchange(): lax.all_to_all(rows.reshape(count, 1, width), ('wide', 'lev'), split_axis...]
    pallas_call x2 -> x1, Pallas kernels: 12.2 us -> 4.43 us  [shards(): pl.pallas_call(inverse_kernel, name='legendre_inverse', out_shape=(jax.Sh...]
    all_to_all x1 -> x0, waiting for transfers between devices: 5.82 us -> none  [exchange(): lax.all_to_all(rows.reshape(count, 1, width), ('wide', 'lev'), split_axis...]
  transfers between devices with their start and end apart: 1 -> 0, of which waited for: 1 -> 0; matrix products, arithmetic and copies ran while one was open for 0% -> 0% of each run, Pallas kernels for 12% -> 0%
where the time goes in v4:
time: 57 us; the launch traced here: 56.9 us
  blocking collectives  46.5 us (82%)
  Pallas kernels  9.69 us (17%)
  between operations  0.66 us (1%)
    all_to_all x2, blocking collectives, exchange(): lax.all_to_all(rows.reshape(count, 1, width), ('wide', 'lev'), split_axis...  46.5 us
    pallas_call x1, Pallas kernels, shards(): pl.pallas_call(inverse_kernel, name='legendre_inverse', out_shape=(jax.Sh...  4.43 us
    pallas_call x1, Pallas kernels, shards(): pl.pallas_call(fourier_kernel, name='fourier', out_shape=(jax.ShapeDtypeS...  3.04 us
    pallas_call x1, Pallas kernels, shards(): pl.pallas_call(direct_kernel, name='legendre_direct', out_shape=jax.Shape...  2.23 us

profile of v4, /device:TPU:1, one launch (start us, length us, event | category | flops | bytes accessed | tf_op | source)
XLA Modules:
  0.0 56.9 jit_solution(2435299439105487034)
XLA Ops:
  0.6 0.0 copy-start
  0.6 4.4 %legendre_inverse.1 = (f32[256,128]{1,0:T(8,128)S(1)}, bf16[5,641,1280]{2,1,0:T(8,128)(2,1)S(1)}, bf16[5,128,1280]{2,1,0:T(8,128)(2,1)S(1)}, f32[200,128]{1,0:T(...) custom-call(s32[640]{0:T(1024)} %wave_hbm.1, s32[5,128]{1,0:T(8,128)} %bitcast.16, ...), custom_call_target="tpu_custom_call" | custom-call | tf_op jit(solution)/shard_map/legendre_inverse/pallas_call | solution.py:404
  5.1 28.3 %all_to_all.10 = f32[256,1,128]{2,1,0:T(1,128)S(1)} all-to-all(f32[256,1,128]{2,1,0:T(1,128)S(1)} %bitcast.14), channel_id=1, replica_groups=mesh['wide'=64,'lev'=4] {'wide','lev'}, dimensions={0} | all-to-all | bytes 262144 | tf_op jit(solution)/shard_map/all_to_all | solution.py:384
  33.3 0.0 copy-done
  33.3 3.0 %fourier.1 = (bf16[5,4,2560]{2,1,0:T(4,128)(2,1)}, f32[256,128]{1,0:T(8,128)S(1)}, bf16[5,1280,768]{2,1,0:T(8,128)(2,1)S(1)}) custom-call(f32[256,128]{1,0:T(8,128)S(1)} %bitcast.11, bf16[5,128,1280]{2,1,0:T(8,128)(2,1)S(1)} %get-tuple-element.13.table, f32[200,128]{1,0:T(8,128)S(1)} %get-tuple-element.14.rotors, ...), custom_call_target="tpu_custom_call" | custom-call | tf_op jit(solution)/shard_map/fourier/pallas_call | solution.py:434
  36.4 18.2 %all_to_all.11 = f32[256,1,128]{2,1,0:T(1,128)S(1)} all-to-all(f32[256,1,128]{2,1,0:T(1,128)S(1)} %bitcast.13), channel_id=1, replica_groups=mesh['wide'=64,'lev'=4] {'wide','lev'}, dimensions={0} | all-to-all | bytes 262144 | tf_op jit(solution)/shard_map/all_to_all | solution.py:384
  54.6 2.2 %legendre_direct.1 = f32[5,2,1,641]{3,2,1,0:T(1,128)} custom-call(f32[256,128]{1,0:T(8,128)S(1)} %bitcast.12, s32[16,128]{1,0:T(8,128)S(1)} %get-tuple-element.19.position, f32[8,768]{1,0:T(8,128)S(1)} %get-tuple-element.20.owners, bf16[5,1280,768]{2,1,0:T(8,128)(2,1)S(1)} %get-tuple-element.21.turned), custom_call_target="tpu_custom_call" | custom-call | tf_op jit(solution)/shard_map/legendre_direct/pallas_call | solution.py:456
Async XLA Ops:
  0.6 32.7 %copy-start = (bf16[5,4,2560]{2,1,0:T(4,128)(2,1)S(1)}, bf16[5,4,2560]{2,1,0:T(4,128)(2,1)}, u32[]{:S(2)}) copy-start(bf16[5,4,2560]{2,1,0:T(4,128)(2,1)} %wind_ref.1) | copy-start | bytes 307204

commit v5 on v4

--- a/solution.py
+++ b/solution.py
@@ -11,7 +11,6 @@
 BF16 = jnp.bfloat16
 I32 = jnp.int32
 NT = (((1,), (1,)), ((), ()))
-FLIGHT = 5
 
 
 def iota(shape, axis):
@@ -157,18 +156,13 @@
 
 
 def turn_pair(turned, leg, p):
-    _, coef, lat_total = leg.shape
-    for at in range(0, coef, 128):
-        if at + 128 <= coef:
-            block = leg[p, at : at + 128, :]
-        else:
-            block = jnp.broadcast_to(leg[p, at : at + 1, :], (128, lat_total))
-        turned[p, :, at : at + 128] = block.T
+    for at in range(0, leg.shape[1] - 1, 128):
+        turned[p, :, at : at + 128] = leg[p, at : at + 128, :].T
 
 
 def inverse_kernel(
     wave_hbm, wave_rows_hbm, spec_hbm, lat_hbm, lat_rows_hbm, active_hbm, weight_hbm, leg_hbm,
-    out_ref, leg, table, rotors, perm, position, owners,
+    out_ref, leg, last_rows, table, rotors, perm, position, owners,
     wave_ref, wave_rows_ref, spec_ref, lat_ref, lat_rows_ref, active_ref, weight_ref,
     stack, small_sems, sems,
 ):
@@ -186,12 +180,11 @@
         ),
         small_sems,
     )
-    copies = [pltpu.make_async_copy(leg_hbm.at[p], leg.at[p], sems.at[p]) for p in range(pairs)]
-    for copy in copies[:FLIGHT]:
-        copy.start()
+    copies = start_copies([(leg_hbm.at[p], leg.at[p]) for p in range(pairs)], sems)
     stack[120:128, :] = jnp.zeros((8, 256), F32)
     fill_perm(perm)
     owners[...] = jnp.zeros_like(owners)
+    last_rows[...] = jnp.zeros_like(last_rows)
     for copy in small:
         copy.wait()
     where_from = latitude_table(lat_rows_ref, lat_here)
@@ -213,9 +206,10 @@
         for i in range(p, lat_here, pairs):
             fill_tables(table, rotors, waves, i, lat_ref, active_ref, weight_ref)
         copies[p].wait()
-        if p + FLIGHT < pairs:
-            copies[p + FLIGHT].start()
-        result = jnp.dot(lefts[p], leg[p], preferred_element_type=F32)
+        result = jnp.dot(lefts[p][:, : coef - 1], leg[p, : coef - 1, :], preferred_element_type=F32)
+        last = leg[p, coef - 1 : coef, :].astype(F32)
+        last_rows[p : p + 1, :] = last
+        result = result + lefts[p][:, coef - 1 :].astype(F32) * last
         total = total + result if p % 2 else result
         if p % 2 == 0 and p < pairs - 1:
             continue
@@ -229,7 +223,7 @@
     out_ref[...] = stack[...].T
 
 
-def direct_kernel(recv_ref, position, owners, turned, out_ref):
+def direct_kernel(recv_ref, position, owners, last_rows, turned, leg, out_ref):
     pairs, _, _, coef = out_ref.shape
     lat_total = turned.shape[1]
     lat_here = lat_total // 256
@@ -246,7 +240,13 @@
         left = jnp.concatenate(ordered, 1).astype(BF16)
         for p in group_pairs(group, pairs):
             own = owners[p : p + 1, :coef] > 0.0
-            result = jnp.dot(left, turned[p], preferred_element_type=F32)
+            if p < turned.shape[0]:
+                result = jnp.dot(left, turned[p], preferred_element_type=F32)
+            else:
+                block = leg[p, : coef - 1, :]
+                result = lax.dot_general(left, block, NT, preferred_element_type=F32)
+            last = jnp.sum(left.astype(F32) * last_rows[p : p + 1, :], axis=1, keepdims=True)
+            result = jnp.concatenate([result, jnp.broadcast_to(last, (8, 128))], 1)
             at = 4 * (p % 2)
             for r in range(2):
                 out_ref[p, r, :, :] = jnp.where(
@@ -294,7 +294,9 @@
         return jnp.broadcast_to(rotors[at : at + 1, :], (8, 128))
 
     copies = []
-    for i in range(lat_here):
+    fields, sums_of = {}, {}
+
+    def inverse_stage(i):
         for p in range(blocks):
             cosx = jnp.where(upper, 1.0, rotor(i, p, 0))
             sinx = jnp.where(upper, 0.0, rotor(i, p, 1))
@@ -318,18 +320,26 @@
                     ).astype(BF16)
                 if a < outer // 2 - 1:
                     real, imag = real * cos2 - imag * sin2, real * sin2 + imag * cos2
-        for p in range(i, leg.shape[0], lat_here):
-            turn_pair(turned, leg, p)
+        if i < turned.shape[0]:
+            turn_pair(turned, leg, i)
         values = lax.dot_general(left[i], table[i], NT, preferred_element_type=F32)
         cells = jnp.broadcast_to(rotors[i * blocks * 8 + 6 : i * blocks * 8 + 7, :], point.shape)
         values = jnp.where(point < cells, values, 0.0).astype(BF16).astype(F32)
-        winds = []
         for a in range(outer):
             grid_ref[i, :, a * 128 : (a + 1) * 128] = values[a * 4 : a * 4 + 4, :].astype(BF16)
-            winds.append(wind_ref[i, :, a * 128 : (a + 1) * 128].astype(F32))
-        copies += start_copies([(grid_ref.at[i], grid_hbm.at[i])], sems.at[pl.ds(i, 1)])
+        copies.extend(start_copies([(grid_ref.at[i], grid_hbm.at[i])], sems.at[pl.ds(i, 1)]))
+        fields[i] = values
+
+    def product_stage(i):
+        values = fields[i]
+        winds = [
+            wind_ref[i, :, a * 128 : (a + 1) * 128].astype(F32) for a in range(outer)
+        ]
         product = (values * jnp.concatenate(winds, 0)).astype(BF16)
-        sums = jnp.dot(product, table[i], preferred_element_type=F32)
+        sums_of[i] = jnp.dot(product, table[i], preferred_element_type=F32)
+
+    def direct_stage(i):
+        sums = sums_of[i]
         for p in range(blocks):
             cosx = jnp.where(upper, 1.0, rotor(i, p, 0))
             sinx = jnp.where(upper, 0.0, rotor(i, p, 1))
@@ -352,6 +362,14 @@
             at = (32 + i * 6 + p) * 4
             backs[at : at + 4, :] = both[4:8, :]
 
+    for step in range(lat_here + 2):
+        if step < lat_here:
+            inverse_stage(step)
+        if 1 <= step <= lat_here:
+            product_stage(step - 1)
+        if step >= 2:
+            direct_stage(step - 2)
+
     joined = jnp.concatenate([backs[pl.ds(l, 64, stride=4), :] for l in range(4)], 1)
     spread = lax.dot_general(joined.astype(BF16), perm[...], NT, preferred_element_type=F32)
     for r in range(2):
@@ -401,12 +419,13 @@
         wave_order, wave_rows, spec_in.reshape(pairs, 2, coef), lat_order, lat_rows, active,
         lat_weight, legendre,
     )
-    outgoing, leg_here, table, rotors, perm, position, owners = pl.pallas_call(
+    outgoing, leg_here, last_rows, table, rotors, perm, position, owners = pl.pallas_call(
         inverse_kernel,
         name="legendre_inverse",
         out_shape=(
             jax.ShapeDtypeStruct((devices, 128), F32),
             jax.ShapeDtypeStruct(legendre.shape, BF16),
+            jax.ShapeDtypeStruct((8, lat_total), F32),
             jax.ShapeDtypeStruct((lat_here, 128, 2 * waves), BF16),
             jax.ShapeDtypeStruct((lat_here * waves // 128 * 8, 128), F32),
             jax.ShapeDtypeStruct((512, 512), BF16),
@@ -414,7 +433,7 @@
             jax.ShapeDtypeStruct((8, wide_coef), F32),
         ),
         in_specs=[hbm()] * len(operands),
-        out_specs=(vmem(),) * 7,
+        out_specs=(vmem(),) * 8,
         scratch_shapes=[
             pltpu.SMEM(wave_order.shape, I32),
             pltpu.VMEM(wave_rows.shape, I32),
@@ -437,7 +456,7 @@
         out_shape=(
             jax.ShapeDtypeStruct(wind.shape, BF16),
             jax.ShapeDtypeStruct((devices, 128), F32),
-            jax.ShapeDtypeStruct((pairs, lat_total, wide_coef), BF16),
+            jax.ShapeDtypeStruct((pairs - 1, lat_total, coef - 1), BF16),
         ),
         in_specs=[vmem()] * 6,
         out_specs=(hbm(), vmem(), vmem()),
@@ -457,10 +476,10 @@
         direct_kernel,
         name="legendre_direct",
         out_shape=jax.ShapeDtypeStruct((pairs, 2, 1, coef), F32),
-        in_specs=[vmem()] * 4,
+        in_specs=[vmem()] * 6,
         out_specs=vmem(),
         compiler_params=limit,
-    )(arrived, position, owners, turned)
+    )(arrived, position, owners, last_rows, turned, leg_here)
     return (grid, spec_out)
 
 

time: 57 us -> 56 us (0.982)
  Pallas kernels: 9.69 us -> 8.69 us
    pallas_call x1, Pallas kernels: 3.04 us -> 2.37 us  [shards(): pl.pallas_call(fourier_kernel, name='fourier', out_shape=(jax.ShapeDtypeS...]
where the time goes in v5:
time: 56 us; the launch traced here: 55.8 us
  blocking collectives  46.5 us (83%)
  Pallas kernels  8.69 us (16%)
  between operations  0.66 us (1%)
    all_to_all x2, blocking collectives, exchange(): lax.all_to_all(rows.reshape(count, 1, width), ('wide', 'lev'), split_axis...  46.5 us
    pallas_call x1, Pallas kernels, shards(): pl.pallas_call(inverse_kernel, name='legendre_inverse', out_shape=(jax.Sh...  4.16 us
    pallas_call x1, Pallas kernels, shards(): pl.pallas_call(fourier_kernel, name='fourier', out_shape=(jax.ShapeDtypeS...  2.37 us
    pallas_call x1, Pallas kernels, shards(): pl.pallas_call(direct_kernel, name='legendre_direct', out_shape=jax.Shape...  2.16 us

profile of v5, /device:TPU:1, one launch (start us, length us, event | category | flops | bytes accessed | tf_op | source)
XLA Modules:
  0.0 55.8 jit_solution(7524154990005767959)
XLA Ops:
  0.6 0.0 copy-start
  0.6 4.2 %legendre_inverse.1 = (f32[256,128]{1,0:T(8,128)S(1)}, bf16[5,641,1280]{2,1,0:T(8,128)(2,1)S(1)}, f32[8,1280]{1,0:T(8,128)S(1)}, bf16[5,128,1280]{2,1,0:T(8,128)...) custom-call(s32[640]{0:T(1024)} %wave_hbm.1, ...), custom_call_target="tpu_custom_call" | custom-call | tf_op jit(solution)/shard_map/legendre_inverse/pallas_call | solution.py:422
  4.8 28.3 %all_to_all.10 = f32[256,1,128]{2,1,0:T(1,128)S(1)} all-to-all(f32[256,1,128]{2,1,0:T(1,128)S(1)} %bitcast.13), channel_id=1, replica_groups=mesh['wide'=64,'lev'=4] {'wide','lev'}, dimensions={0} | all-to-all | bytes 262144 | tf_op jit(solution)/shard_map/all_to_all | solution.py:402
  33.1 0.0 copy-done
  33.1 2.4 %fourier.1 = (bf16[5,4,2560]{2,1,0:T(4,128)(2,1)}, f32[256,128]{1,0:T(8,128)S(1)}, bf16[4,1280,640]{2,1,0:T(8,128)(2,1)S(1)}) custom-call(f32[256,128]{1,0:T(8,128)S(1)} %bitcast.11, bf16[5,128,1280]{2,1,0:T(8,128)(2,1)S(1)} %get-tuple-element.14.table, f32[200,128]{1,0:T(8,128)S(1)} %get-tuple-element.15.rotors, ...), custom_call_target="tpu_custom_call" | custom-call | tf_op jit(solution)/shard_map/fourier/pallas_call | solution.py:453
  35.4 18.2 %all_to_all.11 = f32[256,1,128]{2,1,0:T(1,128)S(1)} all-to-all(f32[256,1,128]{2,1,0:T(1,128)S(1)} %bitcast.14), channel_id=1, replica_groups=mesh['wide'=64,'lev'=4] {'wide','lev'}, dimensions={0} | all-to-all | bytes 262144 | tf_op jit(solution)/shard_map/all_to_all | solution.py:402
  53.7 2.2 %legendre_direct.1 = f32[5,2,1,641]{3,2,1,0:T(1,128)} custom-call(f32[256,128]{1,0:T(8,128)S(1)} %bitcast.12, s32[16,128]{1,0:T(8,128)S(1)} %get-tuple-element.20.position, f32[8,768]{1,0:T(8,128)S(1)} %get-tuple-element.21.owners, f32[8,1280]{1,0:T(8,128)S(1)} %get-tuple-element.22.last_rows, bf16[4,1280,640]{2,1,0:T(8,128)(2,1)S(1)} %get-tuple-element.23.turned, ...), custom_call_target="tpu_custom_call" | custom-call | tf_op jit(solution)/shard_map/legendre_direct/pallas_call | solution.py:475
Async XLA Ops:
  0.6 32.4 %copy-start = (bf16[5,4,2560]{2,1,0:T(4,128)(2,1)S(1)}, bf16[5,4,2560]{2,1,0:T(4,128)(2,1)}, u32[]{:S(2)}) copy-start(bf16[5,4,2560]{2,1,0:T(4,128)(2,1)} %wind_ref.1) | copy-start | bytes 307204

commit v6 on v5

--- a/solution.py
+++ b/solution.py
@@ -203,7 +203,7 @@
         lefts.append(jnp.concatenate(idle + used if p % 2 else used + idle, 0).astype(BF16))
     total = None
     for p in range(pairs):
-        for i in range(p, lat_here, pairs):
+        for i in range(3 * p, min(3 * p + 3, lat_here)):
             fill_tables(table, rotors, waves, i, lat_ref, active_ref, weight_ref)
         copies[p].wait()
         result = jnp.dot(lefts[p][:, : coef - 1], leg[p, : coef - 1, :], preferred_element_type=F32)
@@ -228,7 +228,7 @@
     lat_total = turned.shape[1]
     lat_here = lat_total // 256
     rows = recv_ref[...].T
-    for group in range((pairs + 1) // 2):
+    for group in reversed(range((pairs + 1) // 2)):
         tiles = []
         for i in range(lat_here):
             at = i * 24 + group * 8
@@ -325,9 +325,6 @@
         values = lax.dot_general(left[i], table[i], NT, preferred_element_type=F32)
         cells = jnp.broadcast_to(rotors[i * blocks * 8 + 6 : i * blocks * 8 + 7, :], point.shape)
         values = jnp.where(point < cells, values, 0.0).astype(BF16).astype(F32)
-        for a in range(outer):
-            grid_ref[i, :, a * 128 : (a + 1) * 128] = values[a * 4 : a * 4 + 4, :].astype(BF16)
-        copies.extend(start_copies([(grid_ref.at[i], grid_hbm.at[i])], sems.at[pl.ds(i, 1)]))
         fields[i] = values
 
     def product_stage(i):
@@ -340,6 +337,10 @@
 
     def direct_stage(i):
         sums = sums_of[i]
+        values = fields[i]
+        for a in range(outer):
+            grid_ref[i, :, a * 128 : (a + 1) * 128] = values[a * 4 : a * 4 + 4, :].astype(BF16)
+        copies.extend(start_copies([(grid_ref.at[i], grid_hbm.at[i])], sems.at[pl.ds(i, 1)]))
         for p in range(blocks):
             cosx = jnp.where(upper, 1.0, rotor(i, p, 0))
             sinx = jnp.where(upper, 0.0, rotor(i, p, 1))

time: 56 us -> 56 us (level)
  no operation moved by 1% of the time
where the time goes in v6:
time: 56 us; the launch traced here: 55.8 us
  blocking collectives  46.5 us (83%)
  Pallas kernels  8.68 us (16%)
  between operations  0.66 us (1%)
    all_to_all x2, blocking collectives, exchange(): lax.all_to_all(rows.reshape(count, 1, width), ('wide', 'lev'), split_axis...  46.5 us
    pallas_call x1, Pallas kernels, shards(): pl.pallas_call(inverse_kernel, name='legendre_inverse', out_shape=(jax.Sh...  4.17 us
    pallas_call x1, Pallas kernels, shards(): pl.pallas_call(fourier_kernel, name='fourier', out_shape=(jax.ShapeDtypeS...  2.37 us
    pallas_call x1, Pallas kernels, shards(): pl.pallas_call(direct_kernel, name='legendre_direct', out_shape=jax.Shape...  2.14 us

profile of v6, /device:TPU:1, one launch (start us, length us, event | category | flops | bytes accessed | tf_op | source)
XLA Modules:
  0.0 55.8 jit_solution(5352743827955333840)
XLA Ops:
  0.6 0.0 copy-start
  0.6 4.2 %legendre_inverse.1 = (f32[256,128]{1,0:T(8,128)S(1)}, bf16[5,641,1280]{2,1,0:T(8,128)(2,1)S(1)}, f32[8,1280]{1,0:T(8,128)S(1)}, bf16[5,128,1280]{2,1,0:T(8,128)...) custom-call(s32[640]{0:T(1024)} %wave_hbm.1, ...), custom_call_target="tpu_custom_call" | custom-call | tf_op jit(solution)/shard_map/legendre_inverse/pallas_call | solution.py:423
  4.8 28.3 %all_to_all.10 = f32[256,1,128]{2,1,0:T(1,128)S(1)} all-to-all(f32[256,1,128]{2,1,0:T(1,128)S(1)} %bitcast.13), channel_id=1, replica_groups=mesh['wide'=64,'lev'=4] {'wide','lev'}, dimensions={0} | all-to-all | bytes 262144 | tf_op jit(solution)/shard_map/all_to_all | solution.py:403
  33.1 0.0 copy-done
  33.1 2.4 %fourier.1 = (bf16[5,4,2560]{2,1,0:T(4,128)(2,1)}, f32[256,128]{1,0:T(8,128)S(1)}, bf16[4,1280,640]{2,1,0:T(8,128)(2,1)S(1)}) custom-call(f32[256,128]{1,0:T(8,128)S(1)} %bitcast.11, bf16[5,128,1280]{2,1,0:T(8,128)(2,1)S(1)} %get-tuple-element.14.table, f32[200,128]{1,0:T(8,128)S(1)} %get-tuple-element.15.rotors, ...), custom_call_target="tpu_custom_call" | custom-call | tf_op jit(solution)/shard_map/fourier/pallas_call | solution.py:454
  35.5 18.2 %all_to_all.11 = f32[256,1,128]{2,1,0:T(1,128)S(1)} all-to-all(f32[256,1,128]{2,1,0:T(1,128)S(1)} %bitcast.14), channel_id=1, replica_groups=mesh['wide'=64,'lev'=4] {'wide','lev'}, dimensions={0} | all-to-all | bytes 262144 | tf_op jit(solution)/shard_map/all_to_all | solution.py:403
  53.7 2.1 %legendre_direct.1 = f32[5,2,1,641]{3,2,1,0:T(1,128)} custom-call(f32[256,128]{1,0:T(8,128)S(1)} %bitcast.12, s32[16,128]{1,0:T(8,128)S(1)} %get-tuple-element.20.position, f32[8,768]{1,0:T(8,128)S(1)} %get-tuple-element.21.owners, f32[8,1280]{1,0:T(8,128)S(1)} %get-tuple-element.22.last_rows, bf16[4,1280,640]{2,1,0:T(8,128)(2,1)S(1)} %get-tuple-element.23.turned, ...), custom_call_target="tpu_custom_call" | custom-call | tf_op jit(solution)/shard_map/legendre_direct/pallas_call | solution.py:476
Async XLA Ops:
  0.6 32.4 %copy-start = (bf16[5,4,2560]{2,1,0:T(4,128)(2,1)S(1)}, bf16[5,4,2560]{2,1,0:T(4,128)(2,1)}, u32[]{:S(2)}) copy-start(bf16[5,4,2560]{2,1,0:T(4,128)(2,1)} %wind_ref.1) | copy-start | bytes 307204

commit v7 on v6

--- a/solution.py
+++ b/solution.py
@@ -30,9 +30,11 @@
 
 def latitude_table(lat_ref, lat_here):
     halves = []
-    index = iota((8, 128), 1) * lat_here + jnp.minimum(iota((8, 128), 0), lat_here - 1)
+    row = jnp.minimum(iota((8, 128), 0), lat_here - 1)
     for h in range(2):
-        halves.append(pick(lat_ref, h * lat_here, lat_here, index))
+        device = iota((8, 128), 1) + h * 128
+        slot = (((device & 63) << 2) + (device >> 6)) * lat_here + row
+        halves.append(pick(lat_ref, 0, lat_ref.shape[0], slot))
     return jnp.concatenate(halves, 1)
 
 
@@ -68,14 +70,6 @@
     for c in (-1.0 / 3628800, 1.0 / 40320, -1.0 / 720, 1.0 / 24, -0.5, 1.0):
         cosine = cosine * sq + c
     return 1.0 - 2.0 * sine * sine, 2.0 * sine * cosine
-
-
-def fill_perm(perm):
-    for block in range(0, 512, 256):
-        row = iota((256, 512), 0)
-        target = (row & 3) * 128 + (block // 256) * 64 + (row >> 2)
-        hit = target == iota((256, 512), 1)
-        perm[block : block + 256, :] = jnp.where(hit, 1.0, 0.0).astype(BF16)
 
 
 def wave_table(wave_rows_ref, blocks):
@@ -162,7 +156,7 @@
 
 def inverse_kernel(
     wave_hbm, wave_rows_hbm, spec_hbm, lat_hbm, lat_rows_hbm, active_hbm, weight_hbm, leg_hbm,
-    out_ref, leg, last_rows, table, rotors, perm, position, owners,
+    out_ref, leg, last_rows, table, rotors, position, owners,
     wave_ref, wave_rows_ref, spec_ref, lat_ref, lat_rows_ref, active_ref, weight_ref,
     stack, small_sems, sems,
 ):
@@ -182,7 +176,6 @@
     )
     copies = start_copies([(leg_hbm.at[p], leg.at[p]) for p in range(pairs)], sems)
     stack[120:128, :] = jnp.zeros((8, 256), F32)
-    fill_perm(perm)
     owners[...] = jnp.zeros_like(owners)
     last_rows[...] = jnp.zeros_like(last_rows)
     for copy in small:
@@ -257,7 +250,7 @@
 
 
 def fourier_kernel(
-    recv_ref, table, rotors, perm, wind_ref, leg, grid_hbm, out_ref, turned,
+    recv_ref, table, rotors, wind_ref, leg, grid_hbm, out_ref, turned,
     flat, four, left, backs, grid_ref, sems,
 ):
     lat_here, levels, points = wind_ref.shape
@@ -266,24 +259,17 @@
     outer = points // 128
     for h in range(2):
         flat[h * 128 : (h + 1) * 128, :] = recv_ref[h * 128 : (h + 1) * 128, :].T
-    joined = jnp.concatenate(
-        [
-            jnp.concatenate(
-                [
-                    flat[pl.ds(h * 128 + 2 * s + r, 32, stride=4), :]
-                    for s in range(2)
-                    for h in range(2)
-                ],
-                1,
+    low = iota((32, 128), 1) < 64
+    for h in range(2):
+        for r in range(2):
+            even, odd = (flat[pl.ds(h * 128 + 2 * s + r, 32, stride=4), :] for s in range(2))
+            levels_here = (
+                jnp.where(low, even, pltpu.roll(odd, 64, 1)),
+                jnp.where(low, pltpu.roll(even, 64, 1), odd),
             )
-            for r in range(2)
-        ],
-        0,
-    ).astype(BF16)
-    spread = jnp.dot(joined, perm[...], preferred_element_type=F32)
-    for l in range(4):
-        for copy in range(2):
-            four[pl.ds(copy * 4 + l, 64, stride=8), :] = spread[:, l * 128 : (l + 1) * 128]
+            for n, rows in enumerate(levels_here):
+                for copy in range(2):
+                    four[pl.ds(r * 256 + copy * 4 + 2 * h + n, 32, stride=8), :] = rows
     backs[...] = jnp.zeros_like(backs)
     upper = iota((8, 128), 0) < 4
     outer_row = iota((outer * 4, 128), 0) >> 2
@@ -371,15 +357,15 @@
         if step >= 2:
             direct_stage(step - 2)
 
-    joined = jnp.concatenate([backs[pl.ds(l, 64, stride=4), :] for l in range(4)], 1)
-    spread = lax.dot_general(joined.astype(BF16), perm[...], NT, preferred_element_type=F32)
-    for r in range(2):
-        for s in range(2):
-            for h in range(2):
-                lo = s * 256 + h * 128
-                flat[pl.ds(h * 128 + 2 * s + r, 32, stride=4), :] = spread[
-                    r * 32 : r * 32 + 32, lo : lo + 128
-                ]
+    for h in range(2):
+        for r in range(2):
+            even, odd = (backs[pl.ds(r * 128 + 2 * h + n, 32, stride=4), :] for n in range(2))
+            slots = (
+                jnp.where(low, even, pltpu.roll(odd, 64, 1)),
+                jnp.where(low, pltpu.roll(even, 64, 1), odd),
+            )
+            for s, rows in enumerate(slots):
+                flat[pl.ds(h * 128 + 2 * s + r, 32, stride=4), :] = rows
     for h in range(2):
         out_ref[h * 128 : (h + 1) * 128, :] = flat[h * 128 : (h + 1) * 128, :].T
     for copy in copies:
@@ -401,7 +387,7 @@
 def exchange(rows):
     count, width = rows.shape
     moved = lax.all_to_all(
-        rows.reshape(count, 1, width), ("wide", "lev"), split_axis=0, concat_axis=0, tiled=True
+        rows.reshape(count, 1, width), ("lev", "wide"), split_axis=0, concat_axis=0, tiled=True
     )
     return moved.reshape(count, width)
 
@@ -420,7 +406,7 @@
         wave_order, wave_rows, spec_in.reshape(pairs, 2, coef), lat_order, lat_rows, active,
         lat_weight, legendre,
     )
-    outgoing, leg_here, last_rows, table, rotors, perm, position, owners = pl.pallas_call(
+    outgoing, leg_here, last_rows, table, rotors, position, owners = pl.pallas_call(
         inverse_kernel,
         name="legendre_inverse",
         out_shape=(
@@ -429,12 +415,11 @@
             jax.ShapeDtypeStruct((8, lat_total), F32),
             jax.ShapeDtypeStruct((lat_here, 128, 2 * waves), BF16),
             jax.ShapeDtypeStruct((lat_here * waves // 128 * 8, 128), F32),
-            jax.ShapeDtypeStruct((512, 512), BF16),
             jax.ShapeDtypeStruct((16, 128), I32),
             jax.ShapeDtypeStruct((8, wide_coef), F32),
         ),
         in_specs=[hbm()] * len(operands),
-        out_specs=(vmem(),) * 8,
+        out_specs=(vmem(),) * 7,
         scratch_shapes=[
             pltpu.SMEM(wave_order.shape, I32),
             pltpu.VMEM(wave_rows.shape, I32),
@@ -457,9 +442,9 @@
         out_shape=(
             jax.ShapeDtypeStruct(wind.shape, BF16),
             jax.ShapeDtypeStruct((devices, 128), F32),
-            jax.ShapeDtypeStruct((pairs - 1, lat_total, coef - 1), BF16),
+            jax.ShapeDtypeStruct((3, lat_total, coef - 1), BF16),
         ),
-        in_specs=[vmem()] * 6,
+        in_specs=[vmem()] * 5,
         out_specs=(hbm(), vmem(), vmem()),
         scratch_shapes=[
             pltpu.VMEM((devices, 128), F32),
@@ -470,7 +455,7 @@
             pltpu.SemaphoreType.DMA((lat_here,)),
         ],
         compiler_params=limit,
-    )(arrived, table, rotors, perm, wind, leg_here)
+    )(arrived, table, rotors, wind, leg_here)
 
     arrived = exchange(outgoing)
     spec_out = pl.pallas_call(

time: 56 us -> 56 us (level)
  no operation moved by 1% of the time
where the time goes in v7:
time: 56 us; the launch traced here: 55.9 us
  blocking collectives  46.5 us (83%)
  Pallas kernels  8.75 us (16%)
  between operations  0.66 us (1%)
    all_to_all x2, blocking collectives, exchange(): lax.all_to_all(rows.reshape(count, 1, width), ('lev', 'wide'), split_axis...  46.5 us
    pallas_call x1, Pallas kernels, shards(): pl.pallas_call(inverse_kernel, name='legendre_inverse', out_shape=(jax.Sh...  4.23 us
    pallas_call x1, Pallas kernels, shards(): pl.pallas_call(direct_kernel, name='legendre_direct', out_shape=jax.Shape...  2.35 us
    pallas_call x1, Pallas kernels, shards(): pl.pallas_call(fourier_kernel, name='fourier', out_shape=(jax.ShapeDtypeS...  2.17 us

profile of v7, /device:TPU:1, one launch (start us, length us, event | category | flops | bytes accessed | tf_op | source)
XLA Modules:
  0.0 55.9 jit_solution(9543055419085246606)
XLA Ops:
  0.6 0.0 copy-start
  0.6 4.2 %legendre_inverse.1 = (f32[256,128]{1,0:T(8,128)S(1)}, bf16[5,641,1280]{2,1,0:T(8,128)(2,1)S(1)}, f32[8,1280]{1,0:T(8,128)S(1)}, bf16[5,128,1280]{2,1,0:T(8,128)...) custom-call(s32[640]{0:T(1024)} %wave_hbm.1, s32[5,128]{1,0:T(8,128)} %bitcast.16, ...), custom_call_target="tpu_custom_call" | custom-call | tf_op jit(solution)/shard_map/legendre_inverse/pallas_call | solution.py:409
  4.9 28.3 %all_to_all.10 = f32[256,1,128]{2,1,0:T(1,128)S(1)} all-to-all(f32[256,1,128]{2,1,0:T(1,128)S(1)} %bitcast.13), channel_id=1, replica_groups=mesh['wide'=64,'lev'=4] {'lev','wide'}, dimensions={0} | all-to-all | bytes 262144 | tf_op jit(solution)/shard_map/all_to_all | solution.py:389
  33.2 0.0 copy-done
  33.2 2.2 %fourier.1 = (bf16[5,4,2560]{2,1,0:T(4,128)(2,1)}, f32[256,128]{1,0:T(8,128)S(1)}, bf16[3,1280,640]{2,1,0:T(8,128)(2,1)S(1)}) custom-call(f32[256,128]{1,0:T(8,128)S(1)} %bitcast.12, bf16[5,128,1280]{2,1,0:T(8,128)(2,1)S(1)} %get-tuple-element.13.table, f32[200,128]{1,0:T(8,128)S(1)} %get-tuple-element.14.rotors, bf16[5,4,2560]{2,1,0:T(4,128)(2,1)S(1)} %copy-done, ...), custom_call_target="tpu_custom_call" | custom-call | tf_op jit(solution)/shard_map/fourier/pallas_call | solution.py:439
  35.4 18.2 %all_to_all.11 = f32[256,1,128]{2,1,0:T(1,128)S(1)} all-to-all(f32[256,1,128]{2,1,0:T(1,128)S(1)} %bitcast.14), channel_id=1, replica_groups=mesh['wide'=64,'lev'=4] {'lev','wide'}, dimensions={0} | all-to-all | bytes 262144 | tf_op jit(solution)/shard_map/all_to_all | solution.py:389
  53.5 2.4 %legendre_direct.1 = f32[5,2,1,641]{3,2,1,0:T(1,128)} custom-call(f32[256,128]{1,0:T(8,128)S(1)} %bitcast.11, s32[16,128]{1,0:T(8,128)S(1)} %get-tuple-element.18.position, f32[8,768]{1,0:T(8,128)S(1)} %get-tuple-element.19.owners, f32[8,1280]{1,0:T(8,128)S(1)} %get-tuple-element.20.last_rows, bf16[3,1280,640]{2,1,0:T(8,128)(2,1)S(1)} %get-tuple-element.21.turned, ...), custom_call_target="tpu_custom_call" | custom-call | tf_op jit(solution)/shard_map/legendre_direct/pallas_call | solution.py:461
Async XLA Ops:
  0.6 32.6 %copy-start = (bf16[5,4,2560]{2,1,0:T(4,128)(2,1)S(1)}, bf16[5,4,2560]{2,1,0:T(4,128)(2,1)}, u32[]{:S(2)}) copy-start(bf16[5,4,2560]{2,1,0:T(4,128)(2,1)} %wind_ref.1) | copy-start | bytes 307204
